TPU v7x, 32 devices: a whole 2x2x4 slice. The times are simulated.
32 devices in a mesh: seq: 32 (over z, y, x, core).
Axes of the slice: x: 2, y: 2, z: 4, core: 2. Of those that a mesh axis runs over, the one named last changes fastest.
Arguments:
- hidden: bfloat16 [4096, 2048], P('seq'), may hold values from -6 to 6
- queries: bfloat16 [4096, 2048], P('seq'), may hold values from -6 to 6
- key_rows: bfloat16 [4096, 512], P('seq'), may hold values from -6 to 6
- grad_out: bfloat16 [4096, 2048], P('seq'), may hold values from -6 to 6
- master_value: float32 [2048, 512], P('seq'), may hold values from -0.125 to 0.125
- adam_first: float32 [2048, 512], P('seq'), may hold values from -12 to 12
- adam_second: float32 [2048, 512], P('seq'), may hold values from 1 to 100
Outputs:
- attention: bfloat16 [4096, 2048], P('seq')
- grad_queries: bfloat16 [4096, 2048], P('seq')
- grad_keys: bfloat16 [4096, 512], P('seq')
- grad_hidden: bfloat16 [4096, 2048], P('seq')
- new_master: float32 [2048, 512], P('seq')
- new_first: float32 [2048, 512], P('seq')
- new_second: float32 [2048, 512], P('seq')
All inputs are finite; a program needn't handle non-finite values.
Results may differ from a plain program's by a relative error of at most 0.02.
Values may be sent and summed in bfloat16 or wider, within the bound.
No kernel may reach another device: no remote copies, remote signals or barrier semaphores. Data moves between devices by JAX's collectives and lax.ppermute only.
A program may use at most 64 MiB of HBM per device.

v0:
```python
import math

import jax
import jax.numpy as jnp
from jax import lax
from jax.sharding import PartitionSpec as P

HQ = 16
HK = 4
DH = 128
WINDOW = 512
OPT_STEP = 10


beta_first = 0.9
beta_second = 0.95
learning = 0.001
decay_rate = 0.1
epsilon = 1e-08


def passed_along(block, axis, distance):
    devices = range(lax.axis_size(axis))
    route = [(i - distance, i) for i in devices if i - distance in devices]
    return lax.ppermute(block, axis, route)


def attend_block(query_blk, grad_blk, key_win, value_win, allowed):
    ratio = HQ // HK
    scale = 1.0 / math.sqrt(DH)
    count = query_blk.shape[0]
    out_parts, dq_parts, dk_parts, dv_parts = ([], [], [], [])
    for group in range(HK):
        low = group * ratio * DH
        high = (group + 1) * ratio * DH
        query_group = query_blk[:, low:high].reshape(count, ratio, DH)
        grad_group = grad_blk[:, low:high].reshape(count, ratio, DH)
        key_group = key_win[:, group * DH : (group + 1) * DH]
        value_group = value_win[:, group * DH : (group + 1) * DH]
        scores = (
            jnp.einsum("trd,sd->trs", query_group, key_group, preferred_element_type=jnp.float32)
            * scale
        )
        scores = jnp.where(allowed[:, None, :], scores, -jnp.inf)
        top = jnp.max(scores, axis=2, keepdims=True)
        expd = jnp.exp(scores - top)
        probs = expd / jnp.sum(expd, axis=2, keepdims=True)
        probs_low = probs.astype(jnp.bfloat16)
        out_group = jnp.einsum(
            "trs,sd->trd", probs_low, value_group, preferred_element_type=jnp.float32
        ).astype(jnp.bfloat16)
        delta = jnp.sum(
            grad_group.astype(jnp.float32) * out_group.astype(jnp.float32), axis=2, keepdims=True
        )
        dprob = jnp.einsum(
            "trd,sd->trs", grad_group, value_group, preferred_element_type=jnp.float32
        )
        dscore = (probs * (dprob - delta)).astype(jnp.bfloat16)
        dq_group = (
            jnp.einsum("trs,sd->trd", dscore, key_group, preferred_element_type=jnp.float32) * scale
        ).astype(jnp.bfloat16)
        dk_group = (
            jnp.einsum("trs,trd->sd", dscore, query_group, preferred_element_type=jnp.float32)
            * scale
        )
        dv_group = jnp.einsum(
            "trs,trd->sd", probs_low, grad_group, preferred_element_type=jnp.float32
        )
        out_parts.append(out_group.reshape(count, ratio * DH))
        dq_parts.append(dq_group.reshape(count, ratio * DH))
        dk_parts.append(dk_group)
        dv_parts.append(dv_group)
    return (
        jnp.concatenate(out_parts, 1),
        jnp.concatenate(dq_parts, 1),
        jnp.concatenate(dk_parts, 1),
        jnp.concatenate(dv_parts, 1),
    )


def shards(hidden, queries, key_rows, grad_out, master_value, adam_first, adam_second):
    tok_rows = hidden.shape[0]
    reach = WINDOW // tok_rows
    position = lax.axis_index("seq")
    weight_low = master_value.astype(jnp.bfloat16)
    weight_full = lax.all_gather(weight_low, "seq", axis=0, tiled=True)
    values = jnp.dot(hidden, weight_full, preferred_element_type=jnp.float32).astype(jnp.bfloat16)
    earlier = []
    for distance in range(1, reach + 1):
        earlier.append(passed_along((key_rows, values), "seq", distance))
    ordered = earlier[::-1]
    key_win = jnp.concatenate([entry[0] for entry in ordered] + [key_rows], 0)
    value_win = jnp.concatenate([entry[1] for entry in ordered] + [values], 0)
    span_rows = (reach + 1) * tok_rows
    key_index = jnp.arange(span_rows, dtype=jnp.int32)
    key_pos = position * tok_rows - WINDOW + key_index
    relative = jnp.arange(tok_rows, dtype=jnp.int32)[:, None] + WINDOW - key_index[None, :]
    allowed = (relative >= 0) & (relative < WINDOW) & (key_pos >= 0)[None, :]
    attention, grad_queries, dk_win, dv_win = attend_block(
        queries, grad_out, key_win, value_win, allowed
    )

    def partial_terms(distance):
        low = (reach - distance) * tok_rows
        return (dk_win[low : low + tok_rows], dv_win[low : low + tok_rows])

    key_total, value_total = partial_terms(0)
    for distance in range(1, reach + 1):
        arrived = passed_along(partial_terms(distance), "seq", -distance)
        key_total = key_total + arrived[0]
        value_total = value_total + arrived[1]
    grad_keys = key_total.astype(jnp.bfloat16)
    d_value = value_total.astype(jnp.bfloat16)
    grad_hidden = lax.dot_general(
        d_value, weight_full, (((1,), (1,)), ((), ())), preferred_element_type=jnp.float32
    ).astype(jnp.bfloat16)
    grad_weight = lax.psum_scatter(
        lax.dot_general(
            hidden, d_value, (((0,), (0,)), ((), ())), preferred_element_type=jnp.float32
        ),
        "seq",
        scatter_dimension=0,
        tiled=True,
    )
    new_first = beta_first * adam_first + (1.0 - beta_first) * grad_weight
    new_second = beta_second * adam_second + (1.0 - beta_second) * grad_weight * grad_weight
    first_hat = new_first / (1.0 - beta_first**OPT_STEP)
    second_hat = new_second / (1.0 - beta_second**OPT_STEP)
    new_master = master_value - learning * (
        first_hat / (jnp.sqrt(second_hat) + epsilon) + decay_rate * master_value
    )
    return (attention, grad_queries, grad_keys, grad_hidden, new_master, new_first, new_second)


def solution(mesh):
    placed = (
        P("seq", None),
        P("seq", None),
        P("seq", None),
        P("seq", None),
        P("seq", None),
        P("seq", None),
        P("seq", None),
    )
    return jax.shard_map(
        shards,
        mesh=mesh,
        in_specs=placed,
        out_specs=(
            P("seq", None),
            P("seq", None),
            P("seq", None),
            P("seq", None),
            P("seq", None),
            P("seq", None),
            P("seq", None),
        ),
        check_vma=False,
    )
```

profile of v0, /device:TPU:6, one launch (start us, length us, event | category | flops | bytes accessed | tf_op | source)
XLA Modules:
  0.0 334.3 jit_solution(691577577510038583)
XLA Ops:
  7.2 3.5 %collective-permute-start.2 = (bf16[128,512]{1,0:T(8,128)(2,1)}, bf16[128,512]{1,0:T(8,128)(2,1)S(1)}, u32[]{:S(2)}, u32[]{:S(2)}) collective-permute-start(bf16[128,512]{1,0:T(8,128)(2,1)} %param.9), channel_id=1, source_target_pairs={{0,2},{1,3},{2,4},{3,5},{4,6},{5,7},{6,8},{7,9},{8,10},{9,11},{10,... | collective-permute-start | bytes 393224 | tf_op jit(solution)/shard_map/ppermute | solution.py:25
  10.8 2.6 collective-permute-start.1
  13.3 3.4 %collective-permute-start = (bf16[128,512]{1,0:T(8,128)(2,1)}, bf16[128,512]{1,0:T(8,128)(2,1)S(1)}, u32[]{:S(2)}, u32[]{:S(2)}) collective-permute-start(bf16[128,512]{1,0:T(8,128)(2,1)} %param.9), channel_id=1, source_target_pairs={{0,4},{1,5},{2,6},{3,7},{4,8},{5,9},{6,10},{7,11},{8,12},{9,13},{1... | collective-permute-start | bytes 393224 | tf_op jit(solution)/shard_map/ppermute | solution.py:25
  16.8 2.6 collective-permute-start.3
  25.7 2.7 fusion.76
  28.4 2.5 fusion.75
  30.9 2.5 fusion.77
  38.0 2.9 collective-permute-start.12
  45.2 2.9 collective-permute-start.13
  48.1 11.6 %collective-permute-done.15 = f32[128,512]{0,1:T(8,128)S(1)} collective-permute-done((f32[128,512]{0,1:T(8,128)S(1)}, f32[128,512]{0,1:T(8,128)S(1)}, u32[]{:S(2)}, u32[]{:S(2)}) %collective-permute-start.15) | collective-permute-done | bytes 262176 | tf_op jit(solution)/shard_map/ppermute | solution.py:25
  59.7 2.8 collective-permute-done.14
  62.5 2.9 collective-permute-done.13
  65.4 2.7 convolution_bitcast_fusion
  68.2 5.3 %copy.270 = f32[2048,512]{1,0:T(8,128)} copy(f32[2048,512]{0,1:T(8,128)} %convolution_bitcast_fusion) | data formatting | bytes 8388608
  73.6 127.5 %reduce-scatter.4.cloned.1.call-done = f32[64,512]{1,0:T(8,128)} async-done(((f32[2048,512]{1,0:T(8,128)}), f32[64,512]{1,0:T(8,128)}) %reduce-scatter.4.cloned.1.call-update) | async-done | bytes 131088 | tf_op jit(solution)/shard_map/reduce_scatter | solution.py:117
  203.0 67.2 %all-gather.2.cloned.1.call-done = bf16[2048,512]{1,0:T(8,128)(2,1)} async-done(((bf16[64,512]{1,0:T(8,128)(2,1)}), bf16[2048,512]{1,0:T(8,128)(2,1)}) %all-gather.2.cloned.1.call-update) | async-done | bytes 2097168 | tf_op jit(solution)/shard_map/all_gather | solution.py:86
  274.6 3.3 collective-permute-start.6
  277.9 4.1 %collective-permute-start.5 = (bf16[128,512]{1,0:T(8,128)(2,1)S(1)}, bf16[128,512]{1,0:T(8,128)(2,1)S(1)}, u32[]{:S(2)}, u32[]{:S(2)}) collective-permute-start(bf16[128,512]{1,0:T(8,128)(2,1)S(1)} %convolution_convert_fusion.5), channel_id=1, source_target_pairs={{0,3},{1,4},{2,5},{3,6},{4,7},{5,8},{6,9},{7,10},{8,11},{9,12},{10... | collective-permute-start | bytes 393224 | tf_op jit(solution)/shard_map/ppermute | solution.py:25
  282.0 2.7 collective-permute-start.4
  286.3 2.6 collective-permute-done.4
  299.2 2.7 collective-permute-start.8
  305.8 2.8 collective-permute-start.9
  311.1 9.3 %collective-permute-done.11 = f32[128,512]{0,1:T(8,128)S(1)} collective-permute-done((f32[128,512]{0,1:T(8,128)}, f32[128,512]{0,1:T(8,128)S(1)}, u32[]{:S(2)}, u32[]{:S(2)}) %collective-permute-start.11) | collective-permute-done | bytes 262176 | tf_op jit(solution)/shard_map/ppermute | solution.py:25
  320.4 2.8 collective-permute-done.10
  (144 shorter events, 43.7 us)
Async XLA Ops:
  7.2 58.3 %copy-start = (bf16[128,2048]{1,0:T(8,128)(2,1)S(1)}, bf16[128,2048]{1,0:T(8,128)(2,1)}, u32[]{:S(2)}) copy-start(bf16[128,2048]{1,0:T(8,128)(2,1)} %param.7) | copy-start | bytes 1572868
  7.2 13.4 %copy-start.22 = (bf16[128,2048]{1,0:T(8,128)(2,1)S(1)}, bf16[128,2048]{1,0:T(8,128)(2,1)}, u32[]{:S(2)}) copy-start(bf16[128,2048]{1,0:T(8,128)(2,1)} %param.10) | copy-start | bytes 1572868
  7.2 193.8 %reduce-scatter.4.cloned.1.call-start = ((), (), s32[]{:S(2)}) async-start(), calls=%async_computation.2 | async-start | bytes 4325376 | tf_op jit(solution)/shard_map/reduce_scatter | solution.py:117
  7.2 16.0 %collective-permute-start.2 = (bf16[128,512]{1,0:T(8,128)(2,1)}, bf16[128,512]{1,0:T(8,128)(2,1)S(1)}, u32[]{:S(2)}, u32[]{:S(2)}) collective-permute-start(bf16[128,512]{1,0:T(8,128)(2,1)} %param.9), channel_id=1, source_target_pairs={{0,2},{1,3},{2,4},{3,5},{4,6},{5,7},{6,8},{7,9},{8,10},{9,11},{10,... | collective-permute-start | bytes 393224 | tf_op jit(solution)/shard_map/ppermute | solution.py:25
  10.8 12.4 %collective-permute-start.1 = (bf16[128,512]{1,0:T(8,128)(2,1)}, bf16[128,512]{1,0:T(8,128)(2,1)S(1)}, u32[]{:S(2)}, u32[]{:S(2)}) collective-permute-start(bf16[128,512]{1,0:T(8,128)(2,1)} %param.9), channel_id=1, source_target_pairs={{0,3},{1,4},{2,5},{3,6},{4,7},{5,8},{6,9},{7,10},{8,11},{9,12},{10... | collective-permute-start | bytes 393224 | tf_op jit(solution)/shard_map/ppermute | solution.py:25
  13.3 9.8 %collective-permute-start = (bf16[128,512]{1,0:T(8,128)(2,1)}, bf16[128,512]{1,0:T(8,128)(2,1)S(1)}, u32[]{:S(2)}, u32[]{:S(2)}) collective-permute-start(bf16[128,512]{1,0:T(8,128)(2,1)} %param.9), channel_id=1, source_target_pairs={{0,4},{1,5},{2,6},{3,7},{4,8},{5,9},{6,10},{7,11},{8,12},{9,13},{1... | collective-permute-start | bytes 393224 | tf_op jit(solution)/shard_map/ppermute | solution.py:25
  16.8 6.5 %collective-permute-start.3 = (bf16[128,512]{1,0:T(8,128)(2,1)}, bf16[128,512]{1,0:T(8,128)(2,1)S(1)}, u32[]{:S(2)}, u32[]{:S(2)}) collective-permute-start(bf16[128,512]{1,0:T(8,128)(2,1)} %param.9), channel_id=1, source_target_pairs={{0,1},{1,2},{2,3},{3,4},{4,5},{5,6},{6,7},{7,8},{8,9},{9,10},{10,1... | collective-permute-start | bytes 393224 | tf_op jit(solution)/shard_map/ppermute | solution.py:25
  22.1 15.3 %copy-start.10 = (bf16[128,512]{0,1:T(8,128)(2,1)}, bf16[128,512]{0,1:T(8,128)(2,1)S(1)}, u32[]{:S(2)}) copy-start(bf16[128,512]{0,1:T(8,128)(2,1)S(1)} %copy.198) | copy-start | bytes 393220
  22.2 12.6 %copy-start.14 = (bf16[128,512]{0,1:T(8,128)(2,1)}, bf16[128,512]{0,1:T(8,128)(2,1)S(1)}, u32[]{:S(2)}) copy-start(bf16[128,512]{0,1:T(8,128)(2,1)S(1)} %copy.202) | copy-start | bytes 393220
  22.4 11.1 %copy-start.20 = (bf16[128,512]{0,1:T(8,128)(2,1)}, bf16[128,512]{0,1:T(8,128)(2,1)S(1)}, u32[]{:S(2)}) copy-start(bf16[128,512]{0,1:T(8,128)(2,1)S(1)} %copy.210) | copy-start | bytes 393220
  38.0 10.1 %collective-permute-start.12 = (f32[128,512]{0,1:T(8,128)S(1)}, f32[128,512]{0,1:T(8,128)S(1)}, u32[]{:S(2)}, u32[]{:S(2)}) collective-permute-start(f32[128,512]{0,1:T(8,128)S(1)} %get-tuple-element.38), channel_id=1, source_target_pairs={{1,0},{2,1},{3,2},{4,3},{5,4},{6,5},{7,6},{8,7},{9,8},{10,9},{11,1... | collective-permute-start | bytes 786440 | tf_op jit(solution)/shard_map/ppermute | solution.py:25
  40.9 18.8 %collective-permute-start.15 = (f32[128,512]{0,1:T(8,128)S(1)}, f32[128,512]{0,1:T(8,128)S(1)}, u32[]{:S(2)}, u32[]{:S(2)}) collective-permute-start(f32[128,512]{0,1:T(8,128)S(1)} %get-tuple-element.39), channel_id=1, source_target_pairs={{4,0},{5,1},{6,2},{7,3},{8,4},{9,5},{10,6},{11,7},{12,8},{13,9},{1... | collective-permute-start | bytes 786440 | tf_op jit(solution)/shard_map/ppermute | solution.py:25
  43.3 19.2 %collective-permute-start.14 = (f32[128,512]{0,1:T(8,128)S(1)}, f32[128,512]{0,1:T(8,128)S(1)}, u32[]{:S(2)}, u32[]{:S(2)}) collective-permute-start(f32[128,512]{0,1:T(8,128)S(1)} %get-tuple-element.40), channel_id=1, source_target_pairs={{3,0},{4,1},{5,2},{6,3},{7,4},{8,5},{9,6},{10,7},{11,8},{12,9},{13... | collective-permute-start | bytes 786440 | tf_op jit(solution)/shard_map/ppermute | solution.py:25
  45.2 20.1 %collective-permute-start.13 = (f32[128,512]{0,1:T(8,128)S(1)}, f32[128,512]{0,1:T(8,128)S(1)}, u32[]{:S(2)}, u32[]{:S(2)}) collective-permute-start(f32[128,512]{0,1:T(8,128)S(1)} %get-tuple-element.41), channel_id=1, source_target_pairs={{2,0},{3,1},{4,2},{5,3},{6,4},{7,5},{8,6},{9,7},{10,8},{11,9},{12,... | collective-permute-start | bytes 786440 | tf_op jit(solution)/shard_map/ppermute | solution.py:25
  73.5 196.7 %all-gather.2.cloned.1.call-start = ((), (), s32[]{:S(2)}) async-start(), calls=%async_computation.1 | async-start | bytes 2162688 | tf_op jit(solution)/shard_map/all_gather | solution.py:86
  270.2 14.4 %copy-start.1 = (bf16[2048,512]{1,0:T(8,128)(2,1)S(1)}, bf16[2048,512]{1,0:T(8,128)(2,1)}, u32[]{:S(2)}) copy-start(bf16[2048,512]{1,0:T(8,128)(2,1)} %all-gather.2.cloned.1.call-done) | copy-start | bytes 6291460
  272.4 16.5 %collective-permute-start.7 = (bf16[128,512]{1,0:T(8,128)(2,1)S(1)}, bf16[128,512]{1,0:T(8,128)(2,1)S(1)}, u32[]{:S(2)}, u32[]{:S(2)}) collective-permute-start(bf16[128,512]{1,0:T(8,128)(2,1)S(1)} %convolution_convert_fusion.5), channel_id=1, source_target_pairs={{0,1},{1,2},{2,3},{3,4},{4,5},{5,6},{6,7},{7,8},{8,9},{9,10},{10,1... | collective-permute-start | bytes 393224 | tf_op jit(solution)/shard_map/ppermute | solution.py:25
  274.6 14.3 %collective-permute-start.6 = (bf16[128,512]{1,0:T(8,128)(2,1)S(1)}, bf16[128,512]{1,0:T(8,128)(2,1)S(1)}, u32[]{:S(2)}, u32[]{:S(2)}) collective-permute-start(bf16[128,512]{1,0:T(8,128)(2,1)S(1)} %convolution_convert_fusion.5), channel_id=1, source_target_pairs={{0,2},{1,3},{2,4},{3,5},{4,6},{5,7},{6,8},{7,9},{8,10},{9,11},{10,... | collective-permute-start | bytes 393224 | tf_op jit(solution)/shard_map/ppermute | solution.py:25
  277.9 10.9 %collective-permute-start.5 = (bf16[128,512]{1,0:T(8,128)(2,1)S(1)}, bf16[128,512]{1,0:T(8,128)(2,1)S(1)}, u32[]{:S(2)}, u32[]{:S(2)}) collective-permute-start(bf16[128,512]{1,0:T(8,128)(2,1)S(1)} %convolution_convert_fusion.5), channel_id=1, source_target_pairs={{0,3},{1,4},{2,5},{3,6},{4,7},{5,8},{6,9},{7,10},{8,11},{9,12},{10... | collective-permute-start | bytes 393224 | tf_op jit(solution)/shard_map/ppermute | solution.py:25
  282.0 6.9 %collective-permute-start.4 = (bf16[128,512]{1,0:T(8,128)(2,1)S(1)}, bf16[128,512]{1,0:T(8,128)(2,1)S(1)}, u32[]{:S(2)}, u32[]{:S(2)}) collective-permute-start(bf16[128,512]{1,0:T(8,128)(2,1)S(1)} %convolution_convert_fusion.5), channel_id=1, source_target_pairs={{0,4},{1,5},{2,6},{3,7},{4,8},{5,9},{6,10},{7,11},{8,12},{9,13},{1... | collective-permute-start | bytes 393224 | tf_op jit(solution)/shard_map/ppermute | solution.py:25
  299.2 11.8 %collective-permute-start.8 = (f32[128,512]{0,1:T(8,128)}, f32[128,512]{0,1:T(8,128)S(1)}, u32[]{:S(2)}, u32[]{:S(2)}) collective-permute-start(f32[128,512]{0,1:T(8,128)} %get-tuple-element.42), channel_id=1, source_target_pairs={{1,0},{2,1},{3,2},{4,3},{5,4},{6,5},{7,6},{8,7},{9,8},{10,9},{11,1... | collective-permute-start | bytes 786440 | tf_op jit(solution)/shard_map/ppermute | solution.py:25
  302.0 18.4 %collective-permute-start.11 = (f32[128,512]{0,1:T(8,128)}, f32[128,512]{0,1:T(8,128)S(1)}, u32[]{:S(2)}, u32[]{:S(2)}) collective-permute-start(f32[128,512]{0,1:T(8,128)} %get-tuple-element.43), channel_id=1, source_target_pairs={{4,0},{5,1},{6,2},{7,3},{8,4},{9,5},{10,6},{11,7},{12,8},{13,9},{1... | collective-permute-start | bytes 786440 | tf_op jit(solution)/shard_map/ppermute | solution.py:25
  303.9 19.3 %collective-permute-start.10 = (f32[128,512]{0,1:T(8,128)}, f32[128,512]{0,1:T(8,128)}, u32[]{:S(2)}, u32[]{:S(2)}) collective-permute-start(f32[128,512]{0,1:T(8,128)} %get-tuple-element.44), channel_id=1, source_target_pairs={{3,0},{4,1},{5,2},{6,3},{7,4},{8,5},{9,6},{10,7},{11,8},{12,9},{13... | collective-permute-start | bytes 786440 | tf_op jit(solution)/shard_map/ppermute | solution.py:25
  305.8 19.8 %collective-permute-start.9 = (f32[128,512]{0,1:T(8,128)}, f32[128,512]{0,1:T(8,128)}, u32[]{:S(2)}, u32[]{:S(2)}) collective-permute-start(f32[128,512]{0,1:T(8,128)} %get-tuple-element.45), channel_id=1, source_target_pairs={{2,0},{3,1},{4,2},{5,3},{6,4},{7,5},{8,6},{9,7},{10,8},{11,9},{12,... | collective-permute-start | bytes 786440 | tf_op jit(solution)/shard_map/ppermute | solution.py:25
  (23 other events, 59.7 us)
Sparse Core Ops, SparseCore 0:
  73.6 127.3 reduce-scatter.3
  204.5 65.7 all-gather.1
where the time goes:
time: 335 us; the launch traced here: 334 us
  waiting for transfers between devices  229 us (68%)
  starting transfers between devices  43.9 us (13%)
  matrix products  23.7 us (7%)
  local copies, waits for them, and re-layouts  17.2 us (5%)
  between operations  14.8 us (4%)
  other arithmetic  5.69 us (2%)
    reduce_scatter x1, waiting for transfers between devices, shards(): lax.psum_scatter(lax.dot_general(hidden, d_value, (((0,), (0,)), ((), ())...  127 us
    all_gather x1, waiting for transfers between devices, shards(): weight_full = lax.all_gather(weight_low, 'seq', axis=0, tiled=True)  67.2 us
    ppermute x16, starting transfers between devices, passed_along(): return lax.ppermute(block, axis, route)  43.8 us
    ppermute x16, waiting for transfers between devices, passed_along(): return lax.ppermute(block, axis, route)  34.4 us
    unnamed x72, local copies, waits for them, and re-layouts  12.8 us
    sub x4, matrix products, attend_block(): expd = jnp.exp(scores - top)  9.17 us
  transfers between devices with their start and end apart: 18, of which 10 were waited for; matrix products, arithmetic and copies ran while one was open for 2% of the time, Pallas kernels for 0%

commit v1 on v0

v1 whole, which is shorter than its diff:
```python
import functools
import math

import jax
import jax.numpy as jnp
from jax import lax
from jax.experimental import pallas as pl
from jax.experimental.pallas import tpu as pltpu
from jax.sharding import PartitionSpec as P

HQ = 16
HK = 4
DH = 128
WINDOW = 512
OPT_STEP = 10
RATIO = HQ // HK
LANES = 128

beta_first = 0.9
beta_second = 0.95
learning = 0.001
decay_rate = 0.1
epsilon = 1e-08

BF = jnp.bfloat16
F32 = jnp.float32
MASKED = -1e30


def exchanged(block, mask):
    return lax.ppermute(block, "seq", [(i, i ^ mask) for i in range(lax.axis_size("seq"))])


def passed_along(block, distance):
    devices = range(lax.axis_size("seq"))
    return lax.ppermute(block, "seq", [(i, i + distance) for i in devices if i + distance in devices])


def in_core_order(core, own, other, axis):
    first = jnp.where(core == 0, own, other)
    second = jnp.where(core == 0, other, own)
    return jnp.concatenate([first, second], axis)


def chip_digits(chips):
    digits, shift = [], 0
    while (1 << shift) < chips:
        radix = min(4, chips >> shift)
        digits.append((shift, radix))
        shift += radix.bit_length() - 1
    return digits


def dotted(a, b, contract):
    return lax.dot_general(a, b, (contract, ((), ())), preferred_element_type=F32)


def stacked_heads(block):
    return jnp.concatenate([block[:, h * DH : (h + 1) * DH] for h in range(RATIO)], 0)


def forward_kernel(place, q_own, q_oth, g_own, g_oth, *refs, tok, reach):
    key_refs, (p_ref, *d_refs), acc = refs[: reach + 1], refs[reach + 1 : -1], refs[-1]
    core, chip = place[0], place[1]
    pair = 2 * tok
    span = WINDOW + tok
    keys = jnp.concatenate([ref[...] for ref in key_refs], 0)
    factor = math.log2(math.e) / math.sqrt(DH)
    row = lax.broadcasted_iota(jnp.int32, (tok, RATIO * tok), 0)
    query = lax.rem(lax.broadcasted_iota(jnp.int32, (tok, RATIO * tok), 1), tok)
    index = lax.broadcasted_iota(jnp.int32, (span, 1), 0)
    for b in range(2):
        q = stacked_heads(jnp.where(core == b, q_own[...], q_oth[...]))
        g = stacked_heads(jnp.where(core == b, g_own[...], g_oth[...]))
        s = dotted(keys[b * tok : b * tok + span], q, ((1,), (1,))) * factor
        s = s + jnp.where(index + b * tok + chip * pair >= WINDOW, 0.0, MASKED)
        s = jnp.concatenate(
            [
                jnp.where(row > query, s[:tok], MASKED),
                s[tok:WINDOW],
                jnp.where(row <= query, s[WINDOW:], MASKED),
            ],
            0,
        )
        top = jnp.max(s, axis=0, keepdims=True)
        e = jnp.exp2(s - top)
        p = (e * (1.0 / jnp.sum(e, axis=0, keepdims=True))).astype(BF)
        p_ref[0, b] = p
        d = dotted(p, g, ((1,), (0,)))
        if b == 0:
            acc[:span] = d
        else:
            acc[span:] = d[WINDOW:]
            acc[tok:span] += d[:WINDOW]
    for k, ref in enumerate(d_refs):
        low = (reach - k) * pair
        ref[...] = acc[low : low + pair].astype(ref.dtype)


def backward_kernel(place, q_own, q_oth, g_own, g_oth, *refs, tok, reach):
    key_refs, value_refs = refs[: reach + 1], refs[reach + 1 : 2 * reach + 2]
    p_ref, own_ref, send_ref, *d_refs = refs[2 * reach + 2 : -1]
    acc = refs[-1]
    core = place[0]
    pair = 2 * tok
    span = WINDOW + tok
    keys = jnp.concatenate([ref[...] for ref in key_refs], 0)
    values = jnp.concatenate([ref[...] for ref in value_refs], 0)
    scale = 1.0 / math.sqrt(DH)
    blocks = []
    for b in range(2):
        q = stacked_heads(jnp.where(core == b, q_own[...], q_oth[...]))
        g = stacked_heads(jnp.where(core == b, g_own[...], g_oth[...]))
        k_win = keys[b * tok : b * tok + span]
        v_win = values[b * tok : b * tok + span]
        p = p_ref[0, b]
        out = dotted(v_win, p, ((0,), (0,))).astype(BF)
        delta = jnp.sum(g.T.astype(F32) * out.astype(F32), axis=0, keepdims=True)
        dprob = dotted(v_win, g, ((1,), (1,)))
        dscore = (p.astype(F32) * (dprob - delta)).astype(BF)
        dk = dotted(dscore, q, ((1,), (0,))) * scale
        dq = (dotted(k_win, dscore, ((0,), (0,))) * scale).astype(BF)
        if b == 0:
            acc[:span] = dk
        else:
            acc[span:] = dk[WINDOW:]
            acc[tok:span] += dk[:WINDOW]
        halves = [
            jnp.concatenate([x[:, h * tok : (h + 1) * tok].T for h in range(RATIO)], 1)
            for x in (out, dq)
        ]
        blocks.append(halves)
    for i in range(2):
        own_ref[i] = jnp.where(core == 0, blocks[0][i], blocks[1][i])
        send_ref[i] = jnp.where(core == 0, blocks[1][i], blocks[0][i])
    for k, ref in enumerate(d_refs):
        low = (reach - k) * pair
        ref[...] = acc[low : low + pair].astype(ref.dtype)


def value_kernel(place, h_own, h_oth, *refs, digits, rows):
    pieces, (v_ref, w_ref) = refs[:-2], refs[-2:]
    core, chip = place[0], place[1]
    tok = h_own.shape[0]
    shift = digits[0][1].bit_length() - 1
    for k, piece in enumerate(pieces):
        for z in range(piece.shape[0]):
            target = lax.bitwise_xor(chip, k + (z << shift))
            w_ref[pl.ds(pl.multiple_of(target * rows, rows), rows), :] = piece[z]
    h = jnp.concatenate(
        [jnp.where(core == 0, h_own[...], h_oth[...]), jnp.where(core == 0, h_oth[...], h_own[...])],
        0,
    )
    v_ref[...] = dotted(h, w_ref[...], ((1,), (0,))).astype(BF)


def chip_values(place, hidden, hidden_other, pieces, digits, rows):
    tok, width = hidden.shape
    pair, columns = 2 * tok, pieces[0].shape[-1]
    if rows % 16:
        core, chip = place[0], place[1]
        blocks = jnp.stack(pieces, 1).reshape(-1, rows, columns)
        weight = blocks[jnp.arange(blocks.shape[0]) ^ chip].reshape(width, columns)
        h = in_core_order(core, hidden, hidden_other, 0)
        return dotted(h, weight, ((1,), (0,))).astype(BF), weight
    return pl.pallas_call(
        functools.partial(value_kernel, digits=digits, rows=rows),
        grid_spec=pltpu.PrefetchScalarGridSpec(
            num_scalar_prefetch=1,
            grid=(1,),
            in_specs=[pl.BlockSpec((tok, width), lambda g, s: (0, 0))] * 2
            + [pl.BlockSpec(piece.shape, lambda g, s: (0, 0, 0)) for piece in pieces],
            out_specs=[
                pl.BlockSpec((pair, columns), lambda g, s: (0, 0)),
                pl.BlockSpec((width, columns), lambda g, s: (0, 0)),
            ],
        ),
        out_shape=[
            jax.ShapeDtypeStruct((pair, columns), BF),
            jax.ShapeDtypeStruct((width, columns), BF),
        ],
        cost_estimate=pl.CostEstimate(
            flops=2 * pair * width * columns, bytes_accessed=3 << 20, transcendentals=0
        ),
        name="values",
    )(place, hidden, hidden_other, *pieces)


def shards(hidden, queries, key_rows, grad_out, master_value, adam_first, adam_second):
    tok, width = hidden.shape
    n = lax.axis_size("seq")
    chips = n // 2
    rows = master_value.shape[0]
    pair = 2 * tok
    reach = WINDOW // pair
    kv_half = key_rows.shape[1] // 2
    q_half = queries.shape[1] // 2
    groups = HK // 2
    wide = RATIO * DH
    span = WINDOW + tok
    digits = chip_digits(chips)
    index = lax.axis_index("seq")
    core, chip = index % 2, index // 2
    place = jnp.stack([core, chip]).astype(jnp.int32)

    def half(array, which, size):
        return lax.dynamic_slice_in_dim(array, which * size, size, 1)

    key_own = half(key_rows, core, kv_half)
    weight_low = master_value.astype(BF)
    near = exchanged(
        jnp.concatenate([half(key_rows, 1 - core, kv_half), half(weight_low, 1 - core, kv_half)], 0), 1
    )
    keys = [in_core_order(core, key_own, near[:tok], 0)]
    weight_block = in_core_order(core, half(weight_low, core, kv_half), near[tok:], 0)
    other = exchanged(
        jnp.concatenate([half(queries, 1 - core, q_half), half(grad_out, 1 - core, q_half)], 1), 1
    )
    hidden_other = exchanged(hidden, 1)
    for k in range(1, reach + 1):
        keys.append(passed_along(keys[0], 2 * k))

    pieces = [weight_block[None]]
    for shift, radix in digits[::-1]:
        block = jnp.stack(pieces, 1).reshape(-1, 2 * rows, kv_half)
        pieces = [block] + [exchanged(block, k << (shift + 1)) for k in range(1, radix)]

    def window_spec():
        return [pl.BlockSpec((pair, DH), lambda g, s: (0, g)) for _ in range(reach + 1)]

    half_specs = [
        pl.BlockSpec((tok, wide), lambda g, s: (0, groups * s[0] + g)),
        pl.BlockSpec((tok, wide), lambda g, s: (0, g)),
        pl.BlockSpec((tok, wide), lambda g, s: (0, groups * s[0] + g)),
        pl.BlockSpec((tok, wide), lambda g, s: (0, groups + g)),
    ]
    prob_spec = pl.BlockSpec((1, 2, span, RATIO * tok), lambda g, s: (g, 0, 0, 0))
    grad_shapes = [
        jax.ShapeDtypeStruct((pair, kv_half), BF if k else F32) for k in range(reach + 1)
    ]
    window_flops = 2 * groups * 2 * span * RATIO * tok * DH
    probs, *dv_parts = pl.pallas_call(
        functools.partial(forward_kernel, tok=tok, reach=reach),
        grid_spec=pltpu.PrefetchScalarGridSpec(
            num_scalar_prefetch=1,
            grid=(groups,),
            in_specs=half_specs + window_spec()[::-1],
            out_specs=[prob_spec] + window_spec(),
            scratch_shapes=[pltpu.VMEM(((reach + 1) * pair, DH), F32)],
        ),
        out_shape=[jax.ShapeDtypeStruct((groups, 2, span, RATIO * tok), BF)] + grad_shapes,
        cost_estimate=pl.CostEstimate(
            flops=2 * window_flops, bytes_accessed=8 << 20, transcendentals=window_flops // DH
        ),
        name="probs",
    )(place, queries, other, grad_out, other, *keys[::-1])
    dv_arrived = [passed_along(dv_parts[k], -2 * k) for k in range(1, reach + 1)]
    d_value = dv_parts[0]
    for term in dv_arrived:
        d_value = d_value + term
    d_value = d_value.astype(BF)

    hidden_pair = in_core_order(core, hidden, hidden_other, 0)
    total = dotted(hidden_pair, d_value, ((0,), (0,)))
    for shift, radix in digits:
        total = total.reshape(-1, radix, 2 * rows, kv_half)
        digit = (chip >> shift) % radix

        def portion(k):
            return lax.dynamic_index_in_dim(total, digit ^ k, 1, False)

        sent = [exchanged(portion(k).astype(BF), k << (shift + 1)) for k in range(1, radix)]
        kept = portion(0)
        for term in sent:
            kept = kept + term
        total = kept
    total = total.reshape(2, rows, kv_half)
    grad_weight = in_core_order(
        core,
        lax.dynamic_index_in_dim(total, core, 0, False),
        exchanged(lax.dynamic_index_in_dim(total, 1 - core, 0, False), 1),
        1,
    )

    values, weight_half = chip_values(place, hidden, hidden_other, pieces, digits, 2 * rows)
    value_win = [values] + [passed_along(values, 2 * k) for k in range(1, reach + 1)]

    out_specs = [pl.BlockSpec((2, tok, wide), lambda g, s: (0, 0, g))] * 2
    own, send, *dk_parts = pl.pallas_call(
        functools.partial(backward_kernel, tok=tok, reach=reach),
        grid_spec=pltpu.PrefetchScalarGridSpec(
            num_scalar_prefetch=1,
            grid=(groups,),
            in_specs=half_specs + window_spec() + window_spec() + [prob_spec],
            out_specs=out_specs + window_spec(),
            scratch_shapes=[pltpu.VMEM(((reach + 1) * pair, DH), F32)],
        ),
        out_shape=[jax.ShapeDtypeStruct((2, tok, q_half), BF)] * 2 + grad_shapes,
        cost_estimate=pl.CostEstimate(
            flops=4 * window_flops, bytes_accessed=8 << 20, transcendentals=0
        ),
        name="gradients",
    )(place, queries, other, grad_out, other, *keys[::-1], *value_win[::-1], probs)
    dk_arrived = [passed_along(dk_parts[k], -2 * k) for k in range(1, reach + 1)]
    dk = dk_parts[0]
    for term in dk_arrived:
        dk = dk + term
    dk = dk.astype(BF).reshape(2, tok, kv_half)
    arrived = exchanged(send, 1)
    attention = in_core_order(core, own[0], arrived[0], 1)
    grad_queries = in_core_order(core, own[1], arrived[1], 1)
    grad_keys = in_core_order(
        core,
        lax.dynamic_index_in_dim(dk, core, 0, False),
        exchanged(lax.dynamic_index_in_dim(dk, 1 - core, 0, False), 1),
        1,
    )

    d_value = d_value.reshape(2, tok, kv_half)
    hidden_sent = exchanged(
        dotted(lax.dynamic_index_in_dim(d_value, 1 - core, 0, False), weight_half, ((1,), (1,))).astype(BF),
        1,
    )
    grad_hidden = (
        dotted(lax.dynamic_index_in_dim(d_value, core, 0, False), weight_half, ((1,), (1,))) + hidden_sent
    ).astype(BF)

    new_first = beta_first * adam_first + (1.0 - beta_first) * grad_weight
    new_second = beta_second * adam_second + (1.0 - beta_second) * grad_weight * grad_weight
    first_hat = new_first / (1.0 - beta_first**OPT_STEP)
    second_hat = new_second / (1.0 - beta_second**OPT_STEP)
    new_master = master_value - learning * (
        first_hat / (jnp.sqrt(second_hat) + epsilon) + decay_rate * master_value
    )
    return (attention, grad_queries, grad_keys, grad_hidden, new_master, new_first, new_second)


def solution(mesh):
    return jax.shard_map(
        shards,
        mesh=mesh,
        in_specs=(P("seq", None),) * 7,
        out_specs=(P("seq", None),) * 7,
        check_vma=False,
    )
```

time: 335 us -> 107 us (0.32)
  the two profiles are of different devices: /device:TPU:6 before, /device:TPU:0 now
where the time goes in v1:
time: 107 us
  starting transfers between devices  51.9 us (49%)
  waiting for transfers between devices  25.1 us (23%)
  Pallas kernels  15.4 us (14%)
  local copies, waits for them, and re-layouts  5.76 us (5%)
  other arithmetic  5.27 us (5%)
  matrix products  2.23 us (2%)
  between operations  1.17 us (1%)
    ppermute x19, starting transfers between devices, exchanged(): lax.ppermute(block, 'seq', [(i, i ^ mask) for i in range(lax.axis_size('s...  31 us
    ppermute x19, waiting for transfers between devices, exchanged(): lax.ppermute(block, 'seq', [(i, i ^ mask) for i in range(lax.axis_size('s...  25.1 us
    ppermute x8, starting transfers between devices, passed_along(): lax.ppermute(block, 'seq', [(i, i + distance) for i in devices if i + dis...  20.9 us
    pallas_call x1, Pallas kernels, shards(): pl.pallas_call(functools.partial(backward_kernel, tok=tok, reach=reach),...  6.18 us
    pallas_call x1, Pallas kernels, shards(): pl.pallas_call(functools.partial(forward_kernel, tok=tok, reach=reach), g...  5.87 us
    unnamed x44, local copies, waits for them, and re-layouts  3.68 us
    pallas_call x1, Pallas kernels, chip_values(): pl.pallas_call(functools.partial(value_kernel, digits=digits, rows=rows),...  3.34 us
    concatenate x4, other arithmetic, in_core_order(): return jnp.concatenate([first, second], axis)  2.33 us
  transfers between devices with their start and end apart: 27, of which 9 were waited for; matrix products, arithmetic and copies ran while one was open for 6% of the time, Pallas kernels for 14%

profile of v1, /device:TPU:0, one launch (start us, length us, event | category | flops | bytes accessed | tf_op | source)
XLA Modules:
  0.0 106.9 jit_solution(2159864207760100925)
XLA Ops:
  4.2 4.9 %collective-permute-start.7 = (bf16[1,128,256]{2,1,0:T(8,128)(2,1)S(1)}, bf16[1,128,256]{2,1,0:T(8,128)(2,1)S(1)}, u32[]{:S(2)}, u32[]{:S(2)}) collective-permute-start(bf16[1,128,256]{2,1,0:T(8,128)(2,1)S(1)} %get-tuple-element.53), channel_id=1, source_target_pairs={{0,24},{1,25},{2,26},{3,27},{4,28},{5,29},{6,30},{7,31},{8,16},{9,... | collective-permute-start | bytes 196616 | tf_op jit(solution)/shard_map/ppermute | solution.py:31
  10.3 1.5 %collective-permute-done.7 = bf16[1,128,256]{2,1,0:T(8,128)(2,1)S(1)} collective-permute-done((bf16[1,128,256]{2,1,0:T(8,128)(2,1)S(1)}, bf16[1,128,256]{2,1,0:T(8,128)(2,1)S(1)}, u32[]{:S(2)}, u32[]{:S(2)}) %collective-permute-start.7) | collective-permute-done | bytes 65568 | tf_op jit(solution)/shard_map/ppermute | solution.py:31
  11.8 3.2 %collective-permute-done.6 = bf16[1,128,256]{2,1,0:T(8,128)(2,1)S(1)} collective-permute-done((bf16[1,128,256]{2,1,0:T(8,128)(2,1)S(1)}, bf16[1,128,256]{2,1,0:T(8,128)(2,1)S(1)}, u32[]{:S(2)}, u32[]{:S(2)}) %collective-permute-start.6) | collective-permute-done | bytes 65568 | tf_op jit(solution)/shard_map/ppermute | solution.py:31
  15.1 1.6 %collective-permute-start.8 = (bf16[4,128,256]{2,1,0:T(8,128)(2,1)S(1)}, bf16[4,128,256]{2,1,0:T(8,128)(2,1)S(1)}, u32[]{:S(2)}, u32[]{:S(2)}) collective-permute-start(bf16[4,128,256]{2,1,0:T(8,128)(2,1)S(1)} %maximum_bitcast_fusion.refs_0_), channel_id=1, source_target_pairs={{0,2},{1,3},{2,0},{3,1},{4,6},{5,7},{6,4},{7,5},{8,10},{9,11},{10,... | collective-permute-start | bytes 786440 | tf_op jit(solution)/shard_map/ppermute | solution.py:31
  16.6 1.5 %collective-permute-start.9 = (bf16[4,128,256]{2,1,0:T(8,128)(2,1)S(1)}, bf16[4,128,256]{2,1,0:T(8,128)(2,1)S(1)}, u32[]{:S(2)}, u32[]{:S(2)}) collective-permute-start(bf16[4,128,256]{2,1,0:T(8,128)(2,1)S(1)} %maximum_bitcast_fusion.refs_0_), channel_id=1, source_target_pairs={{0,4},{1,5},{2,6},{3,7},{4,0},{5,1},{6,2},{7,3},{8,12},{9,13},{10,... | collective-permute-start | bytes 786440 | tf_op jit(solution)/shard_map/ppermute | solution.py:31
  18.7 5.6 %collective-permute-done.8.refs_1_ = bf16[4,128,256]{2,1,0:T(8,128)(2,1)S(1)} collective-permute-done((bf16[4,128,256]{2,1,0:T(8,128)(2,1)S(1)}, bf16[4,128,256]{2,1,0:T(8,128)(2,1)S(1)}, u32[]{:S(2)}, u32[]{:S(2)}) %collective-permute-start.8) | collective-permute-done | bytes 262176 | tf_op jit(solution)/shard_map/ppermute | solution.py:31
  24.3 3.4 %collective-permute-start.2 = (bf16[256,256]{1,0:T(8,128)(2,1)S(1)}, bf16[256,256]{1,0:T(8,128)(2,1)S(1)}, u32[]{:S(2)}, u32[]{:S(2)}) collective-permute-start(bf16[256,256]{1,0:T(8,128)(2,1)S(1)} %pad_maximum_fusion.3.refs_2_), channel_id=1, source_target_pairs={{0,4},{1,5},{2,6},{3,7},{4,8},{5,9},{6,10},{7,11},{8,12},{9,13},{1... | collective-permute-start | bytes 393224 | tf_op jit(solution)/shard_map/ppermute | solution.py:36
  27.7 3.8 %collective-permute-done.9.refs_2_ = bf16[4,128,256]{2,1,0:T(8,128)(2,1)S(1)} collective-permute-done((bf16[4,128,256]{2,1,0:T(8,128)(2,1)S(1)}, bf16[4,128,256]{2,1,0:T(8,128)(2,1)S(1)}, u32[]{:S(2)}, u32[]{:S(2)}) %collective-permute-start.9) | collective-permute-done | bytes 262176 | tf_op jit(solution)/shard_map/ppermute | solution.py:31
  35.0 3.3 %values.1 = (bf16[256,256]{1,0:T(8,128)(2,1)}, bf16[2048,256]{1,0:T(8,128)(2,1)}) custom-call(s32[2]{0:T(128)} %pad_add_fusion.place, bf16[128,2048]{1,0:T(8,128)(2,1)} %h_own.1, bf16[128,2048]{1,0:T(8,128)(2,1)} %copy-done.3, bf16[4,128,256]{2,1,0:T(8,128)(2,1)} %copy-done.6, bf16[4,128,256]{2,1,0:T(8,128)(2,1)} %copy-done.10, ...), custom_call_target="tpu_custom_call" | custom-call | flops 268435456 | bytes 3145728 | tf_op jit(solution)/shard_map/values/pallas_call | solution.py:166
  38.3 5.1 %collective-permute-start.11 = (bf16[256,256]{1,0:T(8,128)(2,1)}, bf16[256,256]{1,0:T(8,128)(2,1)S(1)}, u32[]{:S(2)}, u32[]{:S(2)}) collective-permute-start(bf16[256,256]{1,0:T(8,128)(2,1)} %get-tuple-element.18.refs_5_), channel_id=1, source_target_pairs={{0,4},{1,5},{2,6},{3,7},{4,8},{5,9},{6,10},{7,11},{8,12},{9,13},{1... | collective-permute-start | bytes 393224 | tf_op jit(solution)/shard_map/ppermute | solution.py:36
  43.5 5.9 %collective-permute-start.12 = (bf16[256,256]{1,0:T(8,128)(2,1)}, bf16[256,256]{1,0:T(8,128)(2,1)S(1)}, u32[]{:S(2)}, u32[]{:S(2)}) collective-permute-start(bf16[256,256]{1,0:T(8,128)(2,1)} %get-tuple-element.18.refs_5_), channel_id=1, source_target_pairs={{0,2},{1,3},{2,4},{3,5},{4,6},{5,7},{6,8},{7,9},{8,10},{9,11},{10,... | collective-permute-start | bytes 393224 | tf_op jit(solution)/shard_map/ppermute | solution.py:36
  50.8 5.9 %probs.1 = (bf16[2,2,640,512]{3,2,1,0:T(8,128)(2,1)}, f32[256,256]{1,0:T(8,128)}, bf16[256,256]{1,0:T(8,128)(2,1)}, bf16[256,256]{1,0:T(8,128)(2,1)}) custom-call(s32[2]{0:T(128)} %pad_add_fusion.place, bf16[128,2048]{1,0:T(8,128)(2,1)} %q_own.3, bf16[128,2048]{1,0:T(8,128)(2,1)} %copy-done.5, bf16[128,2048]{1,0:T(8,128)(2,1)} %g_own.3, ...), custom_call_target="tpu_custom_call" | custom-call | flops 671088640 | bytes 8388608 | tf_op jit(solution)/shard_map/probs/pallas_call | solution.py:242
  58.0 1.3 %collective-permute-start.17 = (bf16[256,256]{1,0:T(8,128)(2,1)}, bf16[256,256]{1,0:T(8,128)(2,1)S(1)}, u32[]{:S(2)}, u32[]{:S(2)}) collective-permute-start(bf16[256,256]{1,0:T(8,128)(2,1)} %get-tuple-element.26), channel_id=1, source_target_pairs={{2,0},{3,1},{4,2},{5,3},{6,4},{7,5},{8,6},{9,7},{10,8},{11,9},{12,... | collective-permute-start | bytes 393224 | tf_op jit(solution)/shard_map/ppermute | solution.py:36
  60.1 6.2 %gradients.1 = (bf16[2,128,1024]{2,1,0:T(8,128)(2,1)}, bf16[2,128,1024]{2,1,0:T(8,128)(2,1)}, f32[256,256]{1,0:T(8,128)}, bf16[256,256]{1,0:T(8,128)(2,1)}, bf16[256,256]{1,0:T(8,128)(2,1)}) custom-call(s32[2]{0:T(128)} %pad_add_fusion.place, bf16[128,2048]{1,0:T(8,128)(2,1)} %q_own.3, bf16[128,2048]{1,0:T(8,128)(2,1)} %copy-done.5, ...), custom_call_target="tpu_custom_call" | custom-call | flops 1342177280 | bytes 8388608 | tf_op jit(solution)/shard_map/gradients/pallas_call | solution.py:289
  66.4 1.3 %collective-permute-start.15 = (bf16[256,256]{1,0:T(8,128)(2,1)}, bf16[256,256]{1,0:T(8,128)(2,1)S(1)}, u32[]{:S(2)}, u32[]{:S(2)}) collective-permute-start(bf16[256,256]{1,0:T(8,128)(2,1)} %get-tuple-element.24), channel_id=1, source_target_pairs={{4,0},{5,1},{6,2},{7,3},{8,4},{9,5},{10,6},{11,7},{12,8},{13,9},{1... | collective-permute-start | bytes 393224 | tf_op jit(solution)/shard_map/ppermute | solution.py:36
  70.7 6.0 %collective-permute-start.22 = (bf16[4,128,256]{2,1,0:T(8,128)(2,1)S(1)}, bf16[4,128,256]{2,1,0:T(8,128)(2,1)S(1)}, u32[]{:S(2)}, u32[]{:S(2)}) collective-permute-start(bf16[4,128,256]{2,1,0:T(8,128)(2,1)S(1)} %get-tuple-element.33), channel_id=1, source_target_pairs={{0,6},{1,7},{2,4},{3,5},{4,2},{5,3},{6,0},{7,1},{8,14},{9,15},{10,... | collective-permute-start | bytes 786440 | tf_op jit(solution)/shard_map/ppermute | solution.py:31
  76.8 1.8 %collective-permute-start.21 = (bf16[4,128,256]{2,1,0:T(8,128)(2,1)S(1)}, bf16[4,128,256]{2,1,0:T(8,128)(2,1)S(1)}, u32[]{:S(2)}, u32[]{:S(2)}) collective-permute-start(bf16[4,128,256]{2,1,0:T(8,128)(2,1)S(1)} %get-tuple-element.34), channel_id=1, source_target_pairs={{0,4},{1,5},{2,6},{3,7},{4,0},{5,1},{6,2},{7,3},{8,12},{9,13},{10,... | collective-permute-start | bytes 786440 | tf_op jit(solution)/shard_map/ppermute | solution.py:31
  78.6 7.8 %collective-permute-start.20 = (bf16[4,128,256]{2,1,0:T(8,128)(2,1)S(1)}, bf16[4,128,256]{2,1,0:T(8,128)(2,1)S(1)}, u32[]{:S(2)}, u32[]{:S(2)}) collective-permute-start(bf16[4,128,256]{2,1,0:T(8,128)(2,1)S(1)} %get-tuple-element.32), channel_id=1, source_target_pairs={{0,2},{1,3},{2,0},{3,1},{4,6},{5,7},{6,4},{7,5},{8,10},{9,11},{10,... | collective-permute-start | bytes 786440 | tf_op jit(solution)/shard_map/ppermute | solution.py:31
  86.6 3.8 %collective-permute-done.21 = bf16[4,128,256]{2,1,0:T(8,128)(2,1)S(1)} collective-permute-done((bf16[4,128,256]{2,1,0:T(8,128)(2,1)S(1)}, bf16[4,128,256]{2,1,0:T(8,128)(2,1)S(1)}, u32[]{:S(2)}, u32[]{:S(2)}) %collective-permute-start.21) | collective-permute-done | bytes 262176 | tf_op jit(solution)/shard_map/ppermute | solution.py:31
  90.3 2.4 %collective-permute-done.20 = bf16[4,128,256]{2,1,0:T(8,128)(2,1)S(1)} collective-permute-done((bf16[4,128,256]{2,1,0:T(8,128)(2,1)S(1)}, bf16[4,128,256]{2,1,0:T(8,128)(2,1)S(1)}, u32[]{:S(2)}, u32[]{:S(2)}) %collective-permute-start.20) | collective-permute-done | bytes 262176 | tf_op jit(solution)/shard_map/ppermute | solution.py:31
  92.9 2.2 %collective-permute-start.25 = (bf16[1,128,256]{2,1,0:T(8,128)(2,1)S(1)}, bf16[1,128,256]{2,1,0:T(8,128)(2,1)S(1)}, u32[]{:S(2)}, u32[]{:S(2)}) collective-permute-start(bf16[1,128,256]{2,1,0:T(8,128)(2,1)S(1)} %get-tuple-element.42), channel_id=1, source_target_pairs={{0,24},{1,25},{2,26},{3,27},{4,28},{5,29},{6,30},{7,31},{8,16},{9,... | collective-permute-start | bytes 196616 | tf_op jit(solution)/shard_map/ppermute | solution.py:31
  95.3 2.1 %collective-permute-start.23 = (bf16[1,128,256]{2,1,0:T(8,128)(2,1)S(1)}, bf16[1,128,256]{2,1,0:T(8,128)(2,1)S(1)}, u32[]{:S(2)}, u32[]{:S(2)}) collective-permute-start(bf16[1,128,256]{2,1,0:T(8,128)(2,1)S(1)} %get-tuple-element.41), channel_id=1, source_target_pairs={{0,8},{1,9},{2,10},{3,11},{4,12},{5,13},{6,14},{7,15},{8,0},{9,1},... | collective-permute-start | bytes 196616 | tf_op jit(solution)/shard_map/ppermute | solution.py:31
  97.4 1.7 %collective-permute-done.25 = bf16[1,128,256]{2,1,0:T(8,128)(2,1)S(1)} collective-permute-done((bf16[1,128,256]{2,1,0:T(8,128)(2,1)S(1)}, bf16[1,128,256]{2,1,0:T(8,128)(2,1)S(1)}, u32[]{:S(2)}, u32[]{:S(2)}) %collective-permute-start.25) | collective-permute-done | bytes 65568 | tf_op jit(solution)/shard_map/ppermute | solution.py:31
  99.0 2.6 %collective-permute-done.24 = bf16[1,128,256]{2,1,0:T(8,128)(2,1)S(1)} collective-permute-done((bf16[1,128,256]{2,1,0:T(8,128)(2,1)S(1)}, bf16[1,128,256]{2,1,0:T(8,128)(2,1)S(1)}, u32[]{:S(2)}, u32[]{:S(2)}) %collective-permute-start.24) | collective-permute-done | bytes 65568 | tf_op jit(solution)/shard_map/ppermute | solution.py:31
  (108 shorter events, 20.9 us)
Async XLA Ops:
  4.2 7.6 %collective-permute-start.7 = (bf16[1,128,256]{2,1,0:T(8,128)(2,1)S(1)}, bf16[1,128,256]{2,1,0:T(8,128)(2,1)S(1)}, u32[]{:S(2)}, u32[]{:S(2)}) collective-permute-start(bf16[1,128,256]{2,1,0:T(8,128)(2,1)S(1)} %get-tuple-element.53), channel_id=1, source_target_pairs={{0,24},{1,25},{2,26},{3,27},{4,28},{5,29},{6,30},{7,31},{8,16},{9,... | collective-permute-start | bytes 196616 | tf_op jit(solution)/shard_map/ppermute | solution.py:31
  9.1 5.9 %collective-permute-start.6 = (bf16[1,128,256]{2,1,0:T(8,128)(2,1)S(1)}, bf16[1,128,256]{2,1,0:T(8,128)(2,1)S(1)}, u32[]{:S(2)}, u32[]{:S(2)}) collective-permute-start(bf16[1,128,256]{2,1,0:T(8,128)(2,1)S(1)} %get-tuple-element.53), channel_id=1, source_target_pairs={{0,16},{1,17},{2,18},{3,19},{4,20},{5,21},{6,22},{7,23},{8,24},{9,... | collective-permute-start | bytes 196616 | tf_op jit(solution)/shard_map/ppermute | solution.py:31
  9.8 39.6 %collective-permute-start = (bf16[128,2048]{1,0:T(8,128)(2,1)S(1)}, bf16[128,2048]{1,0:T(8,128)(2,1)S(1)}, u32[]{:S(2)}, u32[]{:S(2)}) collective-permute-start(bf16[128,2048]{1,0:T(8,128)(2,1)S(1)} %pad_maximum_fusion), channel_id=1, source_target_pairs={{0,1},{1,0},{2,3},{3,2},{4,5},{5,4},{6,7},{7,6},{8,9},{9,8},{10,11... | collective-permute-start | bytes 1572872 | tf_op jit(solution)/shard_map/ppermute | solution.py:31
  9.9 23.6 %collective-permute-start.4 = (bf16[128,2048]{1,0:T(8,128)(2,1)S(1)}, bf16[128,2048]{1,0:T(8,128)(2,1)S(1)}, u32[]{:S(2)}, u32[]{:S(2)}) collective-permute-start(bf16[128,2048]{1,0:T(8,128)(2,1)S(1)} %copy-done.1), channel_id=1, source_target_pairs={{0,1},{1,0},{2,3},{3,2},{4,5},{5,4},{6,7},{7,6},{8,9},{9,8},{10,11... | collective-permute-start | bytes 1572872 | tf_op jit(solution)/shard_map/ppermute | solution.py:31
  15.1 9.2 %collective-permute-start.8 = (bf16[4,128,256]{2,1,0:T(8,128)(2,1)S(1)}, bf16[4,128,256]{2,1,0:T(8,128)(2,1)S(1)}, u32[]{:S(2)}, u32[]{:S(2)}) collective-permute-start(bf16[4,128,256]{2,1,0:T(8,128)(2,1)S(1)} %maximum_bitcast_fusion.refs_0_), channel_id=1, source_target_pairs={{0,2},{1,3},{2,0},{3,1},{4,6},{5,7},{6,4},{7,5},{8,10},{9,11},{10,... | collective-permute-start | bytes 786440 | tf_op jit(solution)/shard_map/ppermute | solution.py:31
  16.6 14.9 %collective-permute-start.9 = (bf16[4,128,256]{2,1,0:T(8,128)(2,1)S(1)}, bf16[4,128,256]{2,1,0:T(8,128)(2,1)S(1)}, u32[]{:S(2)}, u32[]{:S(2)}) collective-permute-start(bf16[4,128,256]{2,1,0:T(8,128)(2,1)S(1)} %maximum_bitcast_fusion.refs_0_), channel_id=1, source_target_pairs={{0,4},{1,5},{2,6},{3,7},{4,0},{5,1},{6,2},{7,3},{8,12},{9,13},{10,... | collective-permute-start | bytes 786440 | tf_op jit(solution)/shard_map/ppermute | solution.py:31
  18.1 15.3 %collective-permute-start.10 = (bf16[4,128,256]{2,1,0:T(8,128)(2,1)S(1)}, bf16[4,128,256]{2,1,0:T(8,128)(2,1)S(1)}, u32[]{:S(2)}, u32[]{:S(2)}) collective-permute-start(bf16[4,128,256]{2,1,0:T(8,128)(2,1)S(1)} %maximum_bitcast_fusion.refs_0_), channel_id=1, source_target_pairs={{0,6},{1,7},{2,4},{3,5},{4,2},{5,3},{6,0},{7,1},{8,14},{9,15},{10,... | collective-permute-start | bytes 786440 | tf_op jit(solution)/shard_map/ppermute | solution.py:31
  24.3 25.0 %collective-permute-start.2 = (bf16[256,256]{1,0:T(8,128)(2,1)S(1)}, bf16[256,256]{1,0:T(8,128)(2,1)S(1)}, u32[]{:S(2)}, u32[]{:S(2)}) collective-permute-start(bf16[256,256]{1,0:T(8,128)(2,1)S(1)} %pad_maximum_fusion.3.refs_2_), channel_id=1, source_target_pairs={{0,4},{1,5},{2,6},{3,7},{4,8},{5,9},{6,10},{7,11},{8,12},{9,13},{1... | collective-permute-start | bytes 393224 | tf_op jit(solution)/shard_map/ppermute | solution.py:36
  31.5 17.8 %collective-permute-start.3 = (bf16[256,256]{1,0:T(8,128)(2,1)S(1)}, bf16[256,256]{1,0:T(8,128)(2,1)S(1)}, u32[]{:S(2)}, u32[]{:S(2)}) collective-permute-start(bf16[256,256]{1,0:T(8,128)(2,1)S(1)} %pad_maximum_fusion.3.refs_2_), channel_id=1, source_target_pairs={{0,2},{1,3},{2,4},{3,5},{4,6},{5,7},{6,8},{7,9},{8,10},{9,11},{10,... | collective-permute-start | bytes 393224 | tf_op jit(solution)/shard_map/ppermute | solution.py:36
  38.3 21.1 %collective-permute-start.11 = (bf16[256,256]{1,0:T(8,128)(2,1)}, bf16[256,256]{1,0:T(8,128)(2,1)S(1)}, u32[]{:S(2)}, u32[]{:S(2)}) collective-permute-start(bf16[256,256]{1,0:T(8,128)(2,1)} %get-tuple-element.18.refs_5_), channel_id=1, source_target_pairs={{0,4},{1,5},{2,6},{3,7},{4,8},{5,9},{6,10},{7,11},{8,12},{9,13},{1... | collective-permute-start | bytes 393224 | tf_op jit(solution)/shard_map/ppermute | solution.py:36
  43.5 16.0 %collective-permute-start.12 = (bf16[256,256]{1,0:T(8,128)(2,1)}, bf16[256,256]{1,0:T(8,128)(2,1)S(1)}, u32[]{:S(2)}, u32[]{:S(2)}) collective-permute-start(bf16[256,256]{1,0:T(8,128)(2,1)} %get-tuple-element.18.refs_5_), channel_id=1, source_target_pairs={{0,2},{1,3},{2,4},{3,5},{4,6},{5,7},{6,8},{7,9},{8,10},{9,11},{10,... | collective-permute-start | bytes 393224 | tf_op jit(solution)/shard_map/ppermute | solution.py:36
  56.7 12.3 %collective-permute-start.18 = (bf16[256,256]{1,0:T(8,128)(2,1)}, bf16[256,256]{1,0:T(8,128)(2,1)S(1)}, u32[]{:S(2)}, u32[]{:S(2)}) collective-permute-start(bf16[256,256]{1,0:T(8,128)(2,1)} %get-tuple-element.27), channel_id=1, source_target_pairs={{4,0},{5,1},{6,2},{7,3},{8,4},{9,5},{10,6},{11,7},{12,8},{13,9},{1... | collective-permute-start | bytes 393224 | tf_op jit(solution)/shard_map/ppermute | solution.py:36
  58.0 11.0 %collective-permute-start.17 = (bf16[256,256]{1,0:T(8,128)(2,1)}, bf16[256,256]{1,0:T(8,128)(2,1)S(1)}, u32[]{:S(2)}, u32[]{:S(2)}) collective-permute-start(bf16[256,256]{1,0:T(8,128)(2,1)} %get-tuple-element.26), channel_id=1, source_target_pairs={{2,0},{3,1},{4,2},{5,3},{6,4},{7,5},{8,6},{9,7},{10,8},{11,9},{12,... | collective-permute-start | bytes 393224 | tf_op jit(solution)/shard_map/ppermute | solution.py:36
  66.3 37.5 %collective-permute-start.13 = (bf16[2,128,1024]{2,1,0:T(8,128)(2,1)}, bf16[2,128,1024]{2,1,0:T(8,128)(2,1)S(1)}, u32[]{:S(2)}, u32[]{:S(2)}) collective-permute-start(bf16[2,128,1024]{2,1,0:T(8,128)(2,1)} %get-tuple-element.21), channel_id=1, source_target_pairs={{0,1},{1,0},{2,3},{3,2},{4,5},{5,4},{6,7},{7,6},{8,9},{9,8},{10,11... | collective-permute-start | bytes 1572872 | tf_op jit(solution)/shard_map/ppermute | solution.py:31
  66.4 10.4 %collective-permute-start.15 = (bf16[256,256]{1,0:T(8,128)(2,1)}, bf16[256,256]{1,0:T(8,128)(2,1)S(1)}, u32[]{:S(2)}, u32[]{:S(2)}) collective-permute-start(bf16[256,256]{1,0:T(8,128)(2,1)} %get-tuple-element.24), channel_id=1, source_target_pairs={{4,0},{5,1},{6,2},{7,3},{8,4},{9,5},{10,6},{11,7},{12,8},{13,9},{1... | collective-permute-start | bytes 393224 | tf_op jit(solution)/shard_map/ppermute | solution.py:36
  67.7 10.9 %collective-permute-start.14 = (bf16[256,256]{1,0:T(8,128)(2,1)}, bf16[256,256]{1,0:T(8,128)(2,1)S(1)}, u32[]{:S(2)}, u32[]{:S(2)}) collective-permute-start(bf16[256,256]{1,0:T(8,128)(2,1)} %get-tuple-element.23), channel_id=1, source_target_pairs={{2,0},{3,1},{4,2},{5,3},{6,4},{7,5},{8,6},{9,7},{10,8},{11,9},{12,... | collective-permute-start | bytes 393224 | tf_op jit(solution)/shard_map/ppermute | solution.py:36
  69.6 36.0 %collective-permute-start.19 = (bf16[128,2048]{1,0:T(8,128)(2,1)S(1)}, bf16[128,2048]{1,0:T(8,128)(2,1)S(1)}, u32[]{:S(2)}, u32[]{:S(2)}) collective-permute-start(bf16[128,2048]{1,0:T(8,128)(2,1)S(1)} %convolution_convert_fusion), channel_id=1, source_target_pairs={{0,1},{1,0},{2,3},{3,2},{4,5},{5,4},{6,7},{7,6},{8,9},{9,8},{10,11... | collective-permute-start | bytes 1572872 | tf_op jit(solution)/shard_map/ppermute | solution.py:31
  70.7 15.7 %collective-permute-start.22 = (bf16[4,128,256]{2,1,0:T(8,128)(2,1)S(1)}, bf16[4,128,256]{2,1,0:T(8,128)(2,1)S(1)}, u32[]{:S(2)}, u32[]{:S(2)}) collective-permute-start(bf16[4,128,256]{2,1,0:T(8,128)(2,1)S(1)} %get-tuple-element.33), channel_id=1, source_target_pairs={{0,6},{1,7},{2,4},{3,5},{4,2},{5,3},{6,0},{7,1},{8,14},{9,15},{10,... | collective-permute-start | bytes 786440 | tf_op jit(solution)/shard_map/ppermute | solution.py:31
  76.8 13.6 %collective-permute-start.21 = (bf16[4,128,256]{2,1,0:T(8,128)(2,1)S(1)}, bf16[4,128,256]{2,1,0:T(8,128)(2,1)S(1)}, u32[]{:S(2)}, u32[]{:S(2)}) collective-permute-start(bf16[4,128,256]{2,1,0:T(8,128)(2,1)S(1)} %get-tuple-element.34), channel_id=1, source_target_pairs={{0,4},{1,5},{2,6},{3,7},{4,0},{5,1},{6,2},{7,3},{8,12},{9,13},{10,... | collective-permute-start | bytes 786440 | tf_op jit(solution)/shard_map/ppermute | solution.py:31
  78.6 14.2 %collective-permute-start.20 = (bf16[4,128,256]{2,1,0:T(8,128)(2,1)S(1)}, bf16[4,128,256]{2,1,0:T(8,128)(2,1)S(1)}, u32[]{:S(2)}, u32[]{:S(2)}) collective-permute-start(bf16[4,128,256]{2,1,0:T(8,128)(2,1)S(1)} %get-tuple-element.32), channel_id=1, source_target_pairs={{0,2},{1,3},{2,0},{3,1},{4,6},{5,7},{6,4},{7,5},{8,10},{9,11},{10,... | collective-permute-start | bytes 786440 | tf_op jit(solution)/shard_map/ppermute | solution.py:31
  86.5 8.8 %collective-permute-start.16 = (bf16[128,256]{1,0:T(8,128)(2,1)S(1)}, bf16[128,256]{1,0:T(8,128)(2,1)S(1)}, u32[]{:S(2)}, u32[]{:S(2)}) collective-permute-start(bf16[128,256]{1,0:T(8,128)(2,1)S(1)} %dynamic-slice_bitcast_fusion.1), channel_id=1, source_target_pairs={{0,1},{1,0},{2,3},{3,2},{4,5},{5,4},{6,7},{7,6},{8,9},{9,8},{10,11... | collective-permute-start | bytes 196616 | tf_op jit(solution)/shard_map/ppermute | solution.py:31
  92.9 6.1 %collective-permute-start.25 = (bf16[1,128,256]{2,1,0:T(8,128)(2,1)S(1)}, bf16[1,128,256]{2,1,0:T(8,128)(2,1)S(1)}, u32[]{:S(2)}, u32[]{:S(2)}) collective-permute-start(bf16[1,128,256]{2,1,0:T(8,128)(2,1)S(1)} %get-tuple-element.42), channel_id=1, source_target_pairs={{0,24},{1,25},{2,26},{3,27},{4,28},{5,29},{6,30},{7,31},{8,16},{9,... | collective-permute-start | bytes 196616 | tf_op jit(solution)/shard_map/ppermute | solution.py:31
  95.1 6.5 %collective-permute-start.24 = (bf16[1,128,256]{2,1,0:T(8,128)(2,1)S(1)}, bf16[1,128,256]{2,1,0:T(8,128)(2,1)S(1)}, u32[]{:S(2)}, u32[]{:S(2)}) collective-permute-start(bf16[1,128,256]{2,1,0:T(8,128)(2,1)S(1)} %get-tuple-element.43), channel_id=1, source_target_pairs={{0,16},{1,17},{2,18},{3,19},{4,20},{5,21},{6,22},{7,23},{8,24},{9,... | collective-permute-start | bytes 196616 | tf_op jit(solution)/shard_map/ppermute | solution.py:31
  95.3 6.4 %collective-permute-start.23 = (bf16[1,128,256]{2,1,0:T(8,128)(2,1)S(1)}, bf16[1,128,256]{2,1,0:T(8,128)(2,1)S(1)}, u32[]{:S(2)}, u32[]{:S(2)}) collective-permute-start(bf16[1,128,256]{2,1,0:T(8,128)(2,1)S(1)} %get-tuple-element.41), channel_id=1, source_target_pairs={{0,8},{1,9},{2,10},{3,11},{4,12},{5,13},{6,14},{7,15},{8,0},{9,1},... | collective-permute-start | bytes 196616 | tf_op jit(solution)/shard_map/ppermute | solution.py:31
  (25 other events, 244.7 us)

commit v2 on v1

--- a/solution.py
+++ b/solution.py
@@ -8,13 +8,13 @@
 from jax.experimental.pallas import tpu as pltpu
 from jax.sharding import PartitionSpec as P
 
+
 HQ = 16
 HK = 4
 DH = 128
 WINDOW = 512
 OPT_STEP = 10
 RATIO = HQ // HK
-LANES = 128
 
 beta_first = 0.9
 beta_second = 0.95
@@ -32,8 +32,8 @@
 
 
 def passed_along(block, distance):
-    devices = range(lax.axis_size("seq"))
-    return lax.ppermute(block, "seq", [(i, i + distance) for i in devices if i + distance in devices])
+    n = lax.axis_size("seq")
+    return lax.ppermute(block, "seq", [(i, (i + distance) % n) for i in range(n)])
 
 
 def in_core_order(core, own, other, axis):
@@ -61,7 +61,7 @@
 
 def forward_kernel(place, q_own, q_oth, g_own, g_oth, *refs, tok, reach):
     key_refs, (p_ref, *d_refs), acc = refs[: reach + 1], refs[reach + 1 : -1], refs[-1]
-    core, chip = place[0], place[1]
+    core, chip = place[0] & 1, place[0] >> 1
     pair = 2 * tok
     span = WINDOW + tok
     keys = jnp.concatenate([ref[...] for ref in key_refs], 0)
@@ -101,7 +101,7 @@
     key_refs, value_refs = refs[: reach + 1], refs[reach + 1 : 2 * reach + 2]
     p_ref, own_ref, send_ref, *d_refs = refs[2 * reach + 2 : -1]
     acc = refs[-1]
-    core = place[0]
+    core = place[0] & 1
     pair = 2 * tok
     span = WINDOW + tok
     keys = jnp.concatenate([ref[...] for ref in key_refs], 0)
@@ -140,8 +140,7 @@
 
 def value_kernel(place, h_own, h_oth, *refs, digits, rows):
     pieces, (v_ref, w_ref) = refs[:-2], refs[-2:]
-    core, chip = place[0], place[1]
-    tok = h_own.shape[0]
+    core, chip = place[0] & 1, place[0] >> 1
     shift = digits[0][1].bit_length() - 1
     for k, piece in enumerate(pieces):
         for z in range(piece.shape[0]):
@@ -158,7 +157,7 @@
     tok, width = hidden.shape
     pair, columns = 2 * tok, pieces[0].shape[-1]
     if rows % 16:
-        core, chip = place[0], place[1]
+        core, chip = place[0] & 1, place[0] >> 1
         blocks = jnp.stack(pieces, 1).reshape(-1, rows, columns)
         weight = blocks[jnp.arange(blocks.shape[0]) ^ chip].reshape(width, columns)
         h = in_core_order(core, hidden, hidden_other, 0)
@@ -186,8 +185,8 @@
     )(place, hidden, hidden_other, *pieces)
 
 
-def shards(hidden, queries, key_rows, grad_out, master_value, adam_first, adam_second):
-    tok, width = hidden.shape
+def step(hidden, queries, key_rows, grad_out, master_value, adam_first, adam_second):
+    tok, _ = hidden.shape
     n = lax.axis_size("seq")
     chips = n // 2
     rows = master_value.shape[0]
@@ -200,8 +199,8 @@
     span = WINDOW + tok
     digits = chip_digits(chips)
     index = lax.axis_index("seq")
-    core, chip = index % 2, index // 2
-    place = jnp.stack([core, chip]).astype(jnp.int32)
+    core, chip = index & 1, index >> 1
+    place = index.astype(jnp.int32).reshape(1)
 
     def half(array, which, size):
         return lax.dynamic_slice_in_dim(array, which * size, size, 1)
@@ -221,17 +220,20 @@
         keys.append(passed_along(keys[0], 2 * k))
 
     pieces = [weight_block[None]]
-    for shift, radix in digits[::-1]:
+    for shift, radix in digits[:0:-1]:
         block = jnp.stack(pieces, 1).reshape(-1, 2 * rows, kv_half)
         pieces = [block] + [exchanged(block, k << (shift + 1)) for k in range(1, radix)]
 
+    block = jnp.stack(pieces, 1).reshape(-1, 2 * rows, kv_half)
+    pieces = [block] + [exchanged(block, k << 1) for k in range(1, digits[0][1])]
+
     def window_spec():
         return [pl.BlockSpec((pair, DH), lambda g, s: (0, g)) for _ in range(reach + 1)]
 
     half_specs = [
-        pl.BlockSpec((tok, wide), lambda g, s: (0, groups * s[0] + g)),
+        pl.BlockSpec((tok, wide), lambda g, s: (0, groups * (s[0] & 1) + g)),
         pl.BlockSpec((tok, wide), lambda g, s: (0, g)),
-        pl.BlockSpec((tok, wide), lambda g, s: (0, groups * s[0] + g)),
+        pl.BlockSpec((tok, wide), lambda g, s: (0, groups * (s[0] & 1) + g)),
         pl.BlockSpec((tok, wide), lambda g, s: (0, groups + g)),
     ]
     prob_spec = pl.BlockSpec((1, 2, span, RATIO * tok), lambda g, s: (g, 0, 0, 0))
@@ -262,25 +264,18 @@
 
     hidden_pair = in_core_order(core, hidden, hidden_other, 0)
     total = dotted(hidden_pair, d_value, ((0,), (0,)))
-    for shift, radix in digits:
+    total, *pieces = lax.optimization_barrier((total, *pieces))
+
+    def staged(total, stage):
+        shift, radix = digits[stage]
         total = total.reshape(-1, radix, 2 * rows, kv_half)
-        digit = (chip >> shift) % radix
+        digit = (chip >> shift) & (radix - 1)
 
         def portion(k):
             return lax.dynamic_index_in_dim(total, digit ^ k, 1, False)
 
         sent = [exchanged(portion(k).astype(BF), k << (shift + 1)) for k in range(1, radix)]
-        kept = portion(0)
-        for term in sent:
-            kept = kept + term
-        total = kept
-    total = total.reshape(2, rows, kv_half)
-    grad_weight = in_core_order(
-        core,
-        lax.dynamic_index_in_dim(total, core, 0, False),
-        exchanged(lax.dynamic_index_in_dim(total, 1 - core, 0, False), 1),
-        1,
-    )
+        return portion(0), sent
 
     values, weight_half = chip_values(place, hidden, hidden_other, pieces, digits, 2 * rows)
     value_win = [values] + [passed_along(values, 2 * k) for k in range(1, reach + 1)]
@@ -302,28 +297,45 @@
         name="gradients",
     )(place, queries, other, grad_out, other, *keys[::-1], *value_win[::-1], probs)
     dk_arrived = [passed_along(dk_parts[k], -2 * k) for k in range(1, reach + 1)]
-    dk = dk_parts[0]
+    arrived = exchanged(send, 1)
+    for stage in range(len(digits) - 1):
+        total, terms = staged(total, stage)
+        for term in terms:
+            total = total + term
+    kept, terms = staged(total, len(digits) - 1)
+    attention = in_core_order(core, own[0], arrived[0], 1)
+    grad_queries = in_core_order(core, own[1], arrived[1], 1)
+
+    d_value = d_value.reshape(2, tok, kv_half)
+    part, part_send = [
+        dotted(lax.dynamic_index_in_dim(d_value, which, 0, False), weight_half, ((1,), (1,)))
+        for which in (core, 1 - core)
+    ]
+    part_arrived = exchanged(part_send.astype(BF), 1)
+    part, part_arrived = lax.optimization_barrier((part, part_arrived))
+    grad_hidden = (part + part_arrived).astype(BF)
+
+    kept, dk, attention, grad_queries, grad_hidden, *terms = lax.optimization_barrier(
+        (kept, dk_parts[0], attention, grad_queries, grad_hidden, *terms)
+    )
     for term in dk_arrived:
         dk = dk + term
     dk = dk.astype(BF).reshape(2, tok, kv_half)
-    arrived = exchanged(send, 1)
-    attention = in_core_order(core, own[0], arrived[0], 1)
-    grad_queries = in_core_order(core, own[1], arrived[1], 1)
     grad_keys = in_core_order(
         core,
         lax.dynamic_index_in_dim(dk, core, 0, False),
         exchanged(lax.dynamic_index_in_dim(dk, 1 - core, 0, False), 1),
         1,
     )
-
-    d_value = d_value.reshape(2, tok, kv_half)
-    hidden_sent = exchanged(
-        dotted(lax.dynamic_index_in_dim(d_value, 1 - core, 0, False), weight_half, ((1,), (1,))).astype(BF),
+    for term in terms:
+        kept = kept + term
+    total = kept.reshape(2, rows, kv_half)
+    grad_weight = in_core_order(
+        core,
+        lax.dynamic_index_in_dim(total, core, 0, False),
+        exchanged(lax.dynamic_index_in_dim(total, 1 - core, 0, False), 1),
         1,
     )
-    grad_hidden = (
-        dotted(lax.dynamic_index_in_dim(d_value, core, 0, False), weight_half, ((1,), (1,))) + hidden_sent
-    ).astype(BF)
 
     new_first = beta_first * adam_first + (1.0 - beta_first) * grad_weight
     new_second = beta_second * adam_second + (1.0 - beta_second) * grad_weight * grad_weight
@@ -337,7 +349,7 @@
 
 def solution(mesh):
     return jax.shard_map(
-        shards,
+        step,
         mesh=mesh,
         in_specs=(P("seq", None),) * 7,
         out_specs=(P("seq", None),) * 7,

time: 107 us -> 79.8 us (0.75)
  the two profiles are of different devices: /device:TPU:0 before, /device:TPU:6 now
where the time goes in v2:
time: 79.8 us; the launch traced here: 78.9 us
  starting transfers between devices  29.6 us (37%)
  waiting for transfers between devices  21.3 us (27%)
  Pallas kernels  13.2 us (17%)
  other arithmetic  7.76 us (10%)
  local copies, waits for them, and re-layouts  3.76 us (5%)
  matrix products  2.22 us (3%)
  between operations  1.01 us (1%)
    ppermute x19, starting transfers between devices, exchanged(): lax.ppermute(block, 'seq', [(i, i ^ mask) for i in range(lax.axis_size('s...  19.4 us
    ppermute x19, waiting for transfers between devices, exchanged(): lax.ppermute(block, 'seq', [(i, i ^ mask) for i in range(lax.axis_size('s...  12.9 us
    ppermute x8, starting transfers between devices, passed_along(): lax.ppermute(block, 'seq', [(i, (i + distance) % n) for i in range(n)])  10.2 us
    ppermute x8, waiting for transfers between devices, passed_along(): lax.ppermute(block, 'seq', [(i, (i + distance) % n) for i in range(n)])  8.38 us
    pallas_call x1, Pallas kernels, step(): pl.pallas_call(functools.partial(backward_kernel, tok=tok, reach=reach),...  5.39 us
    pallas_call x1, Pallas kernels, step(): pl.pallas_call(functools.partial(forward_kernel, tok=tok, reach=reach), g...  5.16 us
    pallas_call x1, Pallas kernels, chip_values(): pl.pallas_call(functools.partial(value_kernel, digits=digits, rows=rows),...  2.69 us
    concatenate x4, other arithmetic, in_core_order(): return jnp.concatenate([first, second], axis)  2.33 us
  transfers between devices with their start and end apart: 27, of which 8 were waited for; matrix products, arithmetic and copies ran while one was open for 13% of the time, Pallas kernels for 13%

profile of v2, /device:TPU:6, one launch (start us, length us, event | category | flops | bytes accessed | tf_op | source)
XLA Modules:
  0.0 78.9 jit_solution(9702419637350527397)
XLA Ops:
  2.6 1.1 %constant_dynamic-slice_fusion.3 = (bf16[128,1024]{1,0:T(8,128)(2,1)S(1)}, bf16[128,1024]{1,0:T(8,128)(2,1)S(1)}) fusion(bf16[128,2048]{1,0:T(8,128)(2,1)} %g_own.3, s32[]{:T(128)S(6)} %select_n.139, bf16[128,2048]{1,0:T(8,128)(2,1)} %q_own.3), kind=kLoop, calls=%fused_computation.62 | loop fusion | bytes 1048580 | tf_op jit(solution)/shard_map/dynamic_slice | solution.py:206
  4.4 1.6 %collective-permute-start.7 = (bf16[1,128,256]{2,1,0:T(8,128)(2,1)S(1)}, bf16[1,128,256]{2,1,0:T(8,128)(2,1)S(1)}, u32[]{:S(2)}, u32[]{:S(2)}) collective-permute-start(bf16[1,128,256]{2,1,0:T(8,128)(2,1)S(1)} %get-tuple-element.83), channel_id=1, source_target_pairs={{0,8},{1,9},{2,10},{3,11},{4,12},{5,13},{6,14},{7,15},{8,0},{9,1},... | collective-permute-start | bytes 196616 | tf_op jit(solution)/shard_map/ppermute | solution.py:31
  6.1 2.6 %collective-permute-start.8 = (bf16[1,128,256]{2,1,0:T(8,128)(2,1)S(1)}, bf16[1,128,256]{2,1,0:T(8,128)(2,1)S(1)}, u32[]{:S(2)}, u32[]{:S(2)}) collective-permute-start(bf16[1,128,256]{2,1,0:T(8,128)(2,1)S(1)} %get-tuple-element.83), channel_id=1, source_target_pairs={{0,16},{1,17},{2,18},{3,19},{4,20},{5,21},{6,22},{7,23},{8,24},{9,... | collective-permute-start | bytes 196616 | tf_op jit(solution)/shard_map/ppermute | solution.py:31
  8.9 1.5 %collective-permute-start.3 = (bf16[256,256]{1,0:T(8,128)(2,1)S(1)}, bf16[256,256]{1,0:T(8,128)(2,1)S(1)}, u32[]{:S(2)}, u32[]{:S(2)}) collective-permute-start(bf16[256,256]{1,0:T(8,128)(2,1)S(1)} %pad_maximum_fusion.3.refs_2_), channel_id=1, source_target_pairs={{0,4},{1,5},{2,6},{3,7},{4,8},{5,9},{6,10},{7,11},{8,12},{9,13},{1... | collective-permute-start | bytes 393224 | tf_op jit(solution)/shard_map/ppermute | solution.py:36
  10.4 8.2 %collective-permute-done.8 = bf16[1,128,256]{2,1,0:T(8,128)(2,1)S(1)} collective-permute-done((bf16[1,128,256]{2,1,0:T(8,128)(2,1)S(1)}, bf16[1,128,256]{2,1,0:T(8,128)(2,1)S(1)}, u32[]{:S(2)}, u32[]{:S(2)}) %collective-permute-start.8) | collective-permute-done | bytes 65568 | tf_op jit(solution)/shard_map/ppermute | solution.py:31
  18.7 2.1 %collective-permute-start.10 = (bf16[4,128,256]{2,1,0:T(8,128)(2,1)S(1)}, bf16[4,128,256]{2,1,0:T(8,128)(2,1)}, u32[]{:S(2)}, u32[]{:S(2)}) collective-permute-start(bf16[4,128,256]{2,1,0:T(8,128)(2,1)S(1)} %maximum_bitcast_fusion.refs_0_), channel_id=1, source_target_pairs={{0,2},{1,3},{2,0},{3,1},{4,6},{5,7},{6,4},{7,5},{8,10},{9,11},{10,... | collective-permute-start | bytes 786440 | tf_op jit(solution)/shard_map/ppermute | solution.py:31
  20.8 3.2 %collective-permute-done.4.refs_1_ = bf16[256,256]{1,0:T(8,128)(2,1)S(1)} collective-permute-done((bf16[256,256]{1,0:T(8,128)(2,1)S(1)}, bf16[256,256]{1,0:T(8,128)(2,1)S(1)}, u32[]{:S(2)}, u32[]{:S(2)}) %collective-permute-start.4) | collective-permute-done | bytes 131104 | tf_op jit(solution)/shard_map/ppermute | solution.py:36
  24.9 5.2 %probs.1 = (bf16[2,2,640,512]{3,2,1,0:T(8,128)(2,1)}, f32[256,256]{1,0:T(8,128)}, bf16[256,256]{1,0:T(8,128)(2,1)}, bf16[256,256]{1,0:T(8,128)(2,1)}) custom-call(s32[1]{0:T(128)} %bitcast.place, bf16[128,2048]{1,0:T(8,128)(2,1)} %q_own.3, bf16[128,2048]{1,0:T(8,128)(2,1)} %copy-done.3, bf16[128,2048]{1,0:T(8,128)(2,1)} %g_own.3, ...), custom_call_target="tpu_custom_call" | custom-call | flops 671088640 | bytes 8388608 | tf_op jit(solution)/shard_map/probs/pallas_call | solution.py:244
  30.0 1.1 %collective-permute-start.5 = (bf16[256,256]{1,0:T(8,128)(2,1)}, bf16[256,256]{1,0:T(8,128)(2,1)S(1)}, u32[]{:S(2)}, u32[]{:S(2)}) collective-permute-start(bf16[256,256]{1,0:T(8,128)(2,1)} %get-tuple-element.34), channel_id=1, source_target_pairs={{0,30},{1,31},{2,0},{3,1},{4,2},{5,3},{6,4},{7,5},{8,6},{9,7},{10,... | collective-permute-start | bytes 393224 | tf_op jit(solution)/shard_map/ppermute | solution.py:36
  31.2 2.4 %collective-permute-start.6 = (bf16[256,256]{1,0:T(8,128)(2,1)}, bf16[256,256]{1,0:T(8,128)(2,1)S(1)}, u32[]{:S(2)}, u32[]{:S(2)}) collective-permute-start(bf16[256,256]{1,0:T(8,128)(2,1)} %get-tuple-element.35), channel_id=1, source_target_pairs={{0,28},{1,29},{2,30},{3,31},{4,0},{5,1},{6,2},{7,3},{8,4},{9,5},{1... | collective-permute-start | bytes 393224 | tf_op jit(solution)/shard_map/ppermute | solution.py:36
  33.6 4.6 %collective-permute-done.5 = bf16[256,256]{1,0:T(8,128)(2,1)S(1)} collective-permute-done((bf16[256,256]{1,0:T(8,128)(2,1)}, bf16[256,256]{1,0:T(8,128)(2,1)S(1)}, u32[]{:S(2)}, u32[]{:S(2)}) %collective-permute-start.5) | collective-permute-done | bytes 131104 | tf_op jit(solution)/shard_map/ppermute | solution.py:36
  39.1 2.7 %values.1 = (bf16[256,256]{1,0:T(8,128)(2,1)}, bf16[2048,256]{1,0:T(8,128)(2,1)}) custom-call(s32[1]{0:T(128)} %bitcast.place, bf16[128,2048]{1,0:T(8,128)(2,1)} %h_own.1, bf16[128,2048]{1,0:T(8,128)(2,1)} %copy-done.2, bf16[4,128,256]{2,1,0:T(8,128)(2,1)} %copy-done.4, bf16[4,128,256]{2,1,0:T(8,128)(2,1)} %collective-permute-done.10.refs_1_, ...), custom_call_target="tpu_custom_call" | custom-call | flops 268435456 | bytes 3145728 | tf_op jit(solution)/shard_map/values/pallas_call | solution.py:165
  41.8 3.2 %collective-permute-start.16 = (bf16[256,256]{1,0:T(8,128)(2,1)}, bf16[256,256]{1,0:T(8,128)(2,1)}, u32[]{:S(2)}, u32[]{:S(2)}) collective-permute-start(bf16[256,256]{1,0:T(8,128)(2,1)} %get-tuple-element.41.refs_5_), channel_id=1, source_target_pairs={{0,4},{1,5},{2,6},{3,7},{4,8},{5,9},{6,10},{7,11},{8,12},{9,13},{1... | collective-permute-start | bytes 393224 | tf_op jit(solution)/shard_map/ppermute | solution.py:36
  46.1 1.7 %collective-permute-start.13 = (bf16[4,128,256]{2,1,0:T(8,128)(2,1)}, bf16[4,128,256]{2,1,0:T(8,128)(2,1)}, u32[]{:S(2)}, u32[]{:S(2)}) collective-permute-start(bf16[4,128,256]{2,1,0:T(8,128)(2,1)} %get-tuple-element.62), channel_id=1, source_target_pairs={{0,2},{1,3},{2,0},{3,1},{4,6},{5,7},{6,4},{7,5},{8,10},{9,11},{10,... | collective-permute-start | bytes 786440 | tf_op jit(solution)/shard_map/ppermute | solution.py:31
  47.9 1.7 %collective-permute-start.15 = (bf16[4,128,256]{2,1,0:T(8,128)(2,1)S(1)}, bf16[4,128,256]{2,1,0:T(8,128)(2,1)}, u32[]{:S(2)}, u32[]{:S(2)}) collective-permute-start(bf16[4,128,256]{2,1,0:T(8,128)(2,1)S(1)} %get-tuple-element.63), channel_id=1, source_target_pairs={{0,6},{1,7},{2,4},{3,5},{4,2},{5,3},{6,0},{7,1},{8,14},{9,15},{10,... | collective-permute-start | bytes 786440 | tf_op jit(solution)/shard_map/ppermute | solution.py:31
  50.1 1.3 %convolution_convert_fusion = bf16[128,2048]{1,0:T(8,128)(2,1)} fusion(bf16[2048,256]{1,0:T(8,128)(2,1)S(1)} %copy-done, bf16[2,128,256]{2,1,0:T(8,128)(2,1)S(1)} %bitcast.64, s32[]{:T(128)S(6)} %select_n.163), kind=kOutput, calls=%fused_computation | convolution fusion | flops 134479872 | bytes 1638404 | tf_op jit(solution)/shard_map/dot_general | solution.py:55
  51.6 5.4 %gradients.1 = (bf16[2,128,1024]{2,1,0:T(8,128)(2,1)}, bf16[2,128,1024]{2,1,0:T(8,128)(2,1)}, f32[256,256]{1,0:T(8,128)}, bf16[256,256]{1,0:T(8,128)(2,1)}, bf16[256,256]{1,0:T(8,128)(2,1)}) custom-call(s32[1]{0:T(128)} %bitcast.place, bf16[128,2048]{1,0:T(8,128)(2,1)} %q_own.3, bf16[128,2048]{1,0:T(8,128)(2,1)} %copy-done.3, bf16[128,2048]{1,0:T(8,128)(2,1)} %g_own.3, ...), custom_call_target="tpu_custom_call" | custom-call | flops 1342177280 | bytes 8388608 | tf_op jit(solution)/shard_map/gradients/pallas_call | solution.py:284
  57.3 1.8 %collective-permute-start.23 = (bf16[256,256]{1,0:T(8,128)(2,1)}, bf16[256,256]{1,0:T(8,128)(2,1)S(1)}, u32[]{:S(2)}, u32[]{:S(2)}) collective-permute-start(bf16[256,256]{1,0:T(8,128)(2,1)} %get-tuple-element.52), channel_id=1, source_target_pairs={{0,30},{1,31},{2,0},{3,1},{4,2},{5,3},{6,4},{7,5},{8,6},{9,7},{10,... | collective-permute-start | bytes 393224 | tf_op jit(solution)/shard_map/ppermute | solution.py:36
  59.1 2.1 %collective-permute-done.14 = bf16[4,128,256]{2,1,0:T(8,128)(2,1)} collective-permute-done((bf16[4,128,256]{2,1,0:T(8,128)(2,1)}, bf16[4,128,256]{2,1,0:T(8,128)(2,1)}, u32[]{:S(2)}, u32[]{:S(2)}) %collective-permute-start.14) | collective-permute-done | bytes 262176 | tf_op jit(solution)/shard_map/ppermute | solution.py:31
  61.2 1.3 %fusion.5 = f32[4,128,256]{2,1,0:T(8,128)S(1)} fusion(bf16[4,128,256]{2,1,0:T(8,128)(2,1)} %collective-permute-done.15, bf16[4,128,256]{2,1,0:T(8,128)(2,1)} %collective-permute-done.14, bf16[4,128,256]{2,1,0:T(8,128)(2,1)} %collective-permute-done.13, f32[4,4,128,256]{3,2,1,0:T(8,128)S(1)} %bitcast.62, s32[]{:T(128)S(6)} %select_n.148), kind=kLoop, calls=%fused_computation.13 | loop fusion | flops 786432 | bytes 1835012 | tf_op jit(solution)/shard_map/add | solution.py:304
  62.5 5.3 %collective-permute-start.20 = (bf16[1,128,256]{2,1,0:T(8,128)(2,1)S(1)}, bf16[1,128,256]{2,1,0:T(8,128)(2,1)S(1)}, u32[]{:S(2)}, u32[]{:S(2)}) collective-permute-start(bf16[1,128,256]{2,1,0:T(8,128)(2,1)S(1)} %get-tuple-element.73), channel_id=1, source_target_pairs={{0,8},{1,9},{2,10},{3,11},{4,12},{5,13},{6,14},{7,15},{8,0},{9,1},... | collective-permute-start | bytes 196616 | tf_op jit(solution)/shard_map/ppermute | solution.py:31
  67.9 1.9 %add_convert_fusion = bf16[128,2048]{1,0:T(8,128)(2,1)} fusion(f32[128,2048]{1,0:T(8,128)S(1)} %fusion.11, bf16[128,2048]{1,0:T(8,128)(2,1)} %collective-permute-done.19), kind=kLoop, calls=%fused_computation.5 | loop fusion | flops 786432 | bytes 2097152 | tf_op jit(solution)/shard_map/convert_element_type | solution.py:316
  69.9 2.4 %collective-permute-start.22 = (bf16[1,128,256]{2,1,0:T(8,128)(2,1)S(1)}, bf16[1,128,256]{2,1,0:T(8,128)(2,1)S(1)}, u32[]{:S(2)}, u32[]{:S(2)}) collective-permute-start(bf16[1,128,256]{2,1,0:T(8,128)(2,1)S(1)} %get-tuple-element.71), channel_id=1, source_target_pairs={{0,24},{1,25},{2,26},{3,27},{4,28},{5,29},{6,30},{7,31},{8,16},{9,... | collective-permute-start | bytes 196616 | tf_op jit(solution)/shard_map/ppermute | solution.py:31
  74.0 1.9 %collective-permute-done.22 = bf16[1,128,256]{2,1,0:T(8,128)(2,1)S(1)} collective-permute-done((bf16[1,128,256]{2,1,0:T(8,128)(2,1)S(1)}, bf16[1,128,256]{2,1,0:T(8,128)(2,1)S(1)}, u32[]{:S(2)}, u32[]{:S(2)}) %collective-permute-start.22) | collective-permute-done | bytes 65568 | tf_op jit(solution)/shard_map/ppermute | solution.py:31
  (95 shorter events, 11.6 us)
Async XLA Ops:
  3.7 20.3 %collective-permute-start.1 = (bf16[128,2048]{1,0:T(8,128)(2,1)S(1)}, bf16[128,2048]{1,0:T(8,128)(2,1)S(1)}, u32[]{:S(2)}, u32[]{:S(2)}) collective-permute-start(bf16[128,2048]{1,0:T(8,128)(2,1)S(1)} %pad_maximum_fusion), channel_id=1, source_target_pairs={{0,1},{1,0},{2,3},{3,2},{4,5},{5,4},{6,7},{7,6},{8,9},{9,8},{10,11... | collective-permute-start | bytes 1572872 | tf_op jit(solution)/shard_map/ppermute | solution.py:31
  4.3 26.9 %collective-permute-start = (bf16[128,2048]{1,0:T(8,128)(2,1)S(1)}, bf16[128,2048]{1,0:T(8,128)(2,1)S(1)}, u32[]{:S(2)}, u32[]{:S(2)}) collective-permute-start(bf16[128,2048]{1,0:T(8,128)(2,1)S(1)} %copy-done.1), channel_id=1, source_target_pairs={{0,1},{1,0},{2,3},{3,2},{4,5},{5,4},{6,7},{7,6},{8,9},{9,8},{10,11... | collective-permute-start | bytes 1572872 | tf_op jit(solution)/shard_map/ppermute | solution.py:31
  4.4 4.5 %collective-permute-start.7 = (bf16[1,128,256]{2,1,0:T(8,128)(2,1)S(1)}, bf16[1,128,256]{2,1,0:T(8,128)(2,1)S(1)}, u32[]{:S(2)}, u32[]{:S(2)}) collective-permute-start(bf16[1,128,256]{2,1,0:T(8,128)(2,1)S(1)} %get-tuple-element.83), channel_id=1, source_target_pairs={{0,8},{1,9},{2,10},{3,11},{4,12},{5,13},{6,14},{7,15},{8,0},{9,1},... | collective-permute-start | bytes 196616 | tf_op jit(solution)/shard_map/ppermute | solution.py:31
  6.1 12.6 %collective-permute-start.8 = (bf16[1,128,256]{2,1,0:T(8,128)(2,1)S(1)}, bf16[1,128,256]{2,1,0:T(8,128)(2,1)S(1)}, u32[]{:S(2)}, u32[]{:S(2)}) collective-permute-start(bf16[1,128,256]{2,1,0:T(8,128)(2,1)S(1)} %get-tuple-element.83), channel_id=1, source_target_pairs={{0,16},{1,17},{2,18},{3,19},{4,20},{5,21},{6,22},{7,23},{8,24},{9,... | collective-permute-start | bytes 196616 | tf_op jit(solution)/shard_map/ppermute | solution.py:31
  8.6 10.0 %collective-permute-start.9 = (bf16[1,128,256]{2,1,0:T(8,128)(2,1)S(1)}, bf16[1,128,256]{2,1,0:T(8,128)(2,1)S(1)}, u32[]{:S(2)}, u32[]{:S(2)}) collective-permute-start(bf16[1,128,256]{2,1,0:T(8,128)(2,1)S(1)} %get-tuple-element.83), channel_id=1, source_target_pairs={{0,24},{1,25},{2,26},{3,27},{4,28},{5,29},{6,30},{7,31},{8,16},{9,... | collective-permute-start | bytes 196616 | tf_op jit(solution)/shard_map/ppermute | solution.py:31
  8.9 11.8 %collective-permute-start.3 = (bf16[256,256]{1,0:T(8,128)(2,1)S(1)}, bf16[256,256]{1,0:T(8,128)(2,1)S(1)}, u32[]{:S(2)}, u32[]{:S(2)}) collective-permute-start(bf16[256,256]{1,0:T(8,128)(2,1)S(1)} %pad_maximum_fusion.3.refs_2_), channel_id=1, source_target_pairs={{0,4},{1,5},{2,6},{3,7},{4,8},{5,9},{6,10},{7,11},{8,12},{9,13},{1... | collective-permute-start | bytes 393224 | tf_op jit(solution)/shard_map/ppermute | solution.py:36
  18.6 5.4 %collective-permute-start.4 = (bf16[256,256]{1,0:T(8,128)(2,1)S(1)}, bf16[256,256]{1,0:T(8,128)(2,1)S(1)}, u32[]{:S(2)}, u32[]{:S(2)}) collective-permute-start(bf16[256,256]{1,0:T(8,128)(2,1)S(1)} %pad_maximum_fusion.3.refs_2_), channel_id=1, source_target_pairs={{0,2},{1,3},{2,4},{3,5},{4,6},{5,7},{6,8},{7,9},{8,10},{9,11},{10,... | collective-permute-start | bytes 393224 | tf_op jit(solution)/shard_map/ppermute | solution.py:36
  18.7 20.3 %collective-permute-start.10 = (bf16[4,128,256]{2,1,0:T(8,128)(2,1)S(1)}, bf16[4,128,256]{2,1,0:T(8,128)(2,1)}, u32[]{:S(2)}, u32[]{:S(2)}) collective-permute-start(bf16[4,128,256]{2,1,0:T(8,128)(2,1)S(1)} %maximum_bitcast_fusion.refs_0_), channel_id=1, source_target_pairs={{0,2},{1,3},{2,0},{3,1},{4,6},{5,7},{6,4},{7,5},{8,10},{9,11},{10,... | collective-permute-start | bytes 786440 | tf_op jit(solution)/shard_map/ppermute | solution.py:31
  20.8 18.3 %collective-permute-start.11 = (bf16[4,128,256]{2,1,0:T(8,128)(2,1)S(1)}, bf16[4,128,256]{2,1,0:T(8,128)(2,1)}, u32[]{:S(2)}, u32[]{:S(2)}) collective-permute-start(bf16[4,128,256]{2,1,0:T(8,128)(2,1)S(1)} %maximum_bitcast_fusion.refs_0_), channel_id=1, source_target_pairs={{0,4},{1,5},{2,6},{3,7},{4,0},{5,1},{6,2},{7,3},{8,12},{9,13},{10,... | collective-permute-start | bytes 786440 | tf_op jit(solution)/shard_map/ppermute | solution.py:31
  24.0 15.0 %collective-permute-start.12 = (bf16[4,128,256]{2,1,0:T(8,128)(2,1)S(1)}, bf16[4,128,256]{2,1,0:T(8,128)(2,1)}, u32[]{:S(2)}, u32[]{:S(2)}) collective-permute-start(bf16[4,128,256]{2,1,0:T(8,128)(2,1)S(1)} %maximum_bitcast_fusion.refs_0_), channel_id=1, source_target_pairs={{0,6},{1,7},{2,4},{3,5},{4,2},{5,3},{6,0},{7,1},{8,14},{9,15},{10,... | collective-permute-start | bytes 786440 | tf_op jit(solution)/shard_map/ppermute | solution.py:31
  30.0 8.2 %collective-permute-start.5 = (bf16[256,256]{1,0:T(8,128)(2,1)}, bf16[256,256]{1,0:T(8,128)(2,1)S(1)}, u32[]{:S(2)}, u32[]{:S(2)}) collective-permute-start(bf16[256,256]{1,0:T(8,128)(2,1)} %get-tuple-element.34), channel_id=1, source_target_pairs={{0,30},{1,31},{2,0},{3,1},{4,2},{5,3},{6,4},{7,5},{8,6},{9,7},{10,... | collective-permute-start | bytes 393224 | tf_op jit(solution)/shard_map/ppermute | solution.py:36
  31.2 7.3 %collective-permute-start.6 = (bf16[256,256]{1,0:T(8,128)(2,1)}, bf16[256,256]{1,0:T(8,128)(2,1)S(1)}, u32[]{:S(2)}, u32[]{:S(2)}) collective-permute-start(bf16[256,256]{1,0:T(8,128)(2,1)} %get-tuple-element.35), channel_id=1, source_target_pairs={{0,28},{1,29},{2,30},{3,31},{4,0},{5,1},{6,2},{7,3},{8,4},{9,5},{1... | collective-permute-start | bytes 393224 | tf_op jit(solution)/shard_map/ppermute | solution.py:36
  41.8 9.6 %collective-permute-start.16 = (bf16[256,256]{1,0:T(8,128)(2,1)}, bf16[256,256]{1,0:T(8,128)(2,1)}, u32[]{:S(2)}, u32[]{:S(2)}) collective-permute-start(bf16[256,256]{1,0:T(8,128)(2,1)} %get-tuple-element.41.refs_5_), channel_id=1, source_target_pairs={{0,4},{1,5},{2,6},{3,7},{4,8},{5,9},{6,10},{7,11},{8,12},{9,13},{1... | collective-permute-start | bytes 393224 | tf_op jit(solution)/shard_map/ppermute | solution.py:36
  44.9 6.7 %collective-permute-start.17 = (bf16[256,256]{1,0:T(8,128)(2,1)}, bf16[256,256]{1,0:T(8,128)(2,1)}, u32[]{:S(2)}, u32[]{:S(2)}) collective-permute-start(bf16[256,256]{1,0:T(8,128)(2,1)} %get-tuple-element.41.refs_5_), channel_id=1, source_target_pairs={{0,2},{1,3},{2,4},{3,5},{4,6},{5,7},{6,8},{7,9},{8,10},{9,11},{10,... | collective-permute-start | bytes 393224 | tf_op jit(solution)/shard_map/ppermute | solution.py:36
  46.1 11.2 %collective-permute-start.13 = (bf16[4,128,256]{2,1,0:T(8,128)(2,1)}, bf16[4,128,256]{2,1,0:T(8,128)(2,1)}, u32[]{:S(2)}, u32[]{:S(2)}) collective-permute-start(bf16[4,128,256]{2,1,0:T(8,128)(2,1)} %get-tuple-element.62), channel_id=1, source_target_pairs={{0,2},{1,3},{2,0},{3,1},{4,6},{5,7},{6,4},{7,5},{8,10},{9,11},{10,... | collective-permute-start | bytes 786440 | tf_op jit(solution)/shard_map/ppermute | solution.py:31
  47.9 13.3 %collective-permute-start.14 = (bf16[4,128,256]{2,1,0:T(8,128)(2,1)}, bf16[4,128,256]{2,1,0:T(8,128)(2,1)}, u32[]{:S(2)}, u32[]{:S(2)}) collective-permute-start(bf16[4,128,256]{2,1,0:T(8,128)(2,1)} %get-tuple-element.64), channel_id=1, source_target_pairs={{0,4},{1,5},{2,6},{3,7},{4,0},{5,1},{6,2},{7,3},{8,12},{9,13},{10,... | collective-permute-start | bytes 786440 | tf_op jit(solution)/shard_map/ppermute | solution.py:31
  47.9 13.3 %collective-permute-start.15 = (bf16[4,128,256]{2,1,0:T(8,128)(2,1)S(1)}, bf16[4,128,256]{2,1,0:T(8,128)(2,1)}, u32[]{:S(2)}, u32[]{:S(2)}) collective-permute-start(bf16[4,128,256]{2,1,0:T(8,128)(2,1)S(1)} %get-tuple-element.63), channel_id=1, source_target_pairs={{0,6},{1,7},{2,4},{3,5},{4,2},{5,3},{6,0},{7,1},{8,14},{9,15},{10,... | collective-permute-start | bytes 786440 | tf_op jit(solution)/shard_map/ppermute | solution.py:31
  51.3 16.5 %collective-permute-start.19 = (bf16[128,2048]{1,0:T(8,128)(2,1)}, bf16[128,2048]{1,0:T(8,128)(2,1)}, u32[]{:S(2)}, u32[]{:S(2)}) collective-permute-start(bf16[128,2048]{1,0:T(8,128)(2,1)} %convolution_convert_fusion), channel_id=1, source_target_pairs={{0,1},{1,0},{2,3},{3,2},{4,5},{5,4},{6,7},{7,6},{8,9},{9,8},{10,11... | collective-permute-start | bytes 1572872 | tf_op jit(solution)/shard_map/ppermute | solution.py:31
  57.0 12.9 %collective-permute-start.18 = (bf16[2,128,1024]{2,1,0:T(8,128)(2,1)}, bf16[2,128,1024]{2,1,0:T(8,128)(2,1)S(1)}, u32[]{:S(2)}, u32[]{:S(2)}) collective-permute-start(bf16[2,128,1024]{2,1,0:T(8,128)(2,1)} %get-tuple-element.45), channel_id=1, source_target_pairs={{0,1},{1,0},{2,3},{3,2},{4,5},{5,4},{6,7},{7,6},{8,9},{9,8},{10,11... | collective-permute-start | bytes 1572872 | tf_op jit(solution)/shard_map/ppermute | solution.py:31
  57.3 18.6 %collective-permute-start.23 = (bf16[256,256]{1,0:T(8,128)(2,1)}, bf16[256,256]{1,0:T(8,128)(2,1)S(1)}, u32[]{:S(2)}, u32[]{:S(2)}) collective-permute-start(bf16[256,256]{1,0:T(8,128)(2,1)} %get-tuple-element.52), channel_id=1, source_target_pairs={{0,30},{1,31},{2,0},{3,1},{4,2},{5,3},{6,4},{7,5},{8,6},{9,7},{10,... | collective-permute-start | bytes 393224 | tf_op jit(solution)/shard_map/ppermute | solution.py:36
  61.2 14.8 %collective-permute-start.24 = (bf16[256,256]{1,0:T(8,128)(2,1)}, bf16[256,256]{1,0:T(8,128)(2,1)S(1)}, u32[]{:S(2)}, u32[]{:S(2)}) collective-permute-start(bf16[256,256]{1,0:T(8,128)(2,1)} %get-tuple-element.53), channel_id=1, source_target_pairs={{0,28},{1,29},{2,30},{3,31},{4,0},{5,1},{6,2},{7,3},{8,4},{9,5},{1... | collective-permute-start | bytes 393224 | tf_op jit(solution)/shard_map/ppermute | solution.py:36
  62.5 11.5 %collective-permute-start.20 = (bf16[1,128,256]{2,1,0:T(8,128)(2,1)S(1)}, bf16[1,128,256]{2,1,0:T(8,128)(2,1)S(1)}, u32[]{:S(2)}, u32[]{:S(2)}) collective-permute-start(bf16[1,128,256]{2,1,0:T(8,128)(2,1)S(1)} %get-tuple-element.73), channel_id=1, source_target_pairs={{0,8},{1,9},{2,10},{3,11},{4,12},{5,13},{6,14},{7,15},{8,0},{9,1},... | collective-permute-start | bytes 196616 | tf_op jit(solution)/shard_map/ppermute | solution.py:31
  67.9 6.2 %collective-permute-start.21 = (bf16[1,128,256]{2,1,0:T(8,128)(2,1)S(1)}, bf16[1,128,256]{2,1,0:T(8,128)(2,1)S(1)}, u32[]{:S(2)}, u32[]{:S(2)}) collective-permute-start(bf16[1,128,256]{2,1,0:T(8,128)(2,1)S(1)} %get-tuple-element.72), channel_id=1, source_target_pairs={{0,16},{1,17},{2,18},{3,19},{4,20},{5,21},{6,22},{7,23},{8,24},{9,... | collective-permute-start | bytes 196616 | tf_op jit(solution)/shard_map/ppermute | solution.py:31
  69.9 6.1 %collective-permute-start.22 = (bf16[1,128,256]{2,1,0:T(8,128)(2,1)S(1)}, bf16[1,128,256]{2,1,0:T(8,128)(2,1)S(1)}, u32[]{:S(2)}, u32[]{:S(2)}) collective-permute-start(bf16[1,128,256]{2,1,0:T(8,128)(2,1)S(1)} %get-tuple-element.71), channel_id=1, source_target_pairs={{0,24},{1,25},{2,26},{3,27},{4,28},{5,29},{6,30},{7,31},{8,16},{9,... | collective-permute-start | bytes 196616 | tf_op jit(solution)/shard_map/ppermute | solution.py:31
  (18 other events, 113.3 us)

commit v3 on v2

--- a/solution.py
+++ b/solution.py
@@ -185,6 +185,13 @@
     )(place, hidden, hidden_other, *pieces)
 
 
+def first_kernel(place, key_ref, weight_ref, out_ref):
+    core = place[0] & 1
+    tok, half = key_ref.shape[0], key_ref.shape[1] // 2
+    out_ref[:tok] = jnp.where(core == 0, key_ref[:, half:], key_ref[:, :half])
+    out_ref[tok:] = jnp.where(core == 0, weight_ref[:, half:], weight_ref[:, :half]).astype(BF)
+
+
 def step(hidden, queries, key_rows, grad_out, master_value, adam_first, adam_second):
     tok, _ = hidden.shape
     n = lax.axis_size("seq")
@@ -208,7 +215,21 @@
     key_own = half(key_rows, core, kv_half)
     weight_low = master_value.astype(BF)
     near = exchanged(
-        jnp.concatenate([half(key_rows, 1 - core, kv_half), half(weight_low, 1 - core, kv_half)], 0), 1
+        pl.pallas_call(
+            first_kernel,
+            grid_spec=pltpu.PrefetchScalarGridSpec(
+                num_scalar_prefetch=1,
+                grid=(1,),
+                in_specs=[
+                    pl.BlockSpec(array.shape, lambda g, s: (0, 0)) for array in (key_rows, master_value)
+                ],
+                out_specs=pl.BlockSpec((tok + rows, kv_half), lambda g, s: (0, 0)),
+            ),
+            out_shape=jax.ShapeDtypeStruct((tok + rows, kv_half), BF),
+            cost_estimate=pl.CostEstimate(flops=0, bytes_accessed=1 << 18, transcendentals=0),
+            name="first",
+        )(place, key_rows, master_value),
+        1,
     )
     keys = [in_core_order(core, key_own, near[:tok], 0)]
     weight_block = in_core_order(core, half(weight_low, core, kv_half), near[tok:], 0)
@@ -246,7 +267,7 @@
         grid_spec=pltpu.PrefetchScalarGridSpec(
             num_scalar_prefetch=1,
             grid=(groups,),
-            in_specs=half_specs + window_spec()[::-1],
+            in_specs=half_specs + window_spec(),
             out_specs=[prob_spec] + window_spec(),
             scratch_shapes=[pltpu.VMEM(((reach + 1) * pair, DH), F32)],
         ),
@@ -263,8 +284,7 @@
     d_value = d_value.astype(BF)
 
     hidden_pair = in_core_order(core, hidden, hidden_other, 0)
-    total = dotted(hidden_pair, d_value, ((0,), (0,)))
-    total, *pieces = lax.optimization_barrier((total, *pieces))
+    total = dotted(hidden_pair, d_value, ((0,), (0,))).astype(BF)
 
     def staged(total, stage):
         shift, radix = digits[stage]
@@ -275,7 +295,7 @@
             return lax.dynamic_index_in_dim(total, digit ^ k, 1, False)
 
         sent = [exchanged(portion(k).astype(BF), k << (shift + 1)) for k in range(1, radix)]
-        return portion(0), sent
+        return portion(0).astype(F32), sent
 
     values, weight_half = chip_values(place, hidden, hidden_other, pieces, digits, 2 * rows)
     value_win = [values] + [passed_along(values, 2 * k) for k in range(1, reach + 1)]
@@ -306,14 +326,13 @@
     attention = in_core_order(core, own[0], arrived[0], 1)
     grad_queries = in_core_order(core, own[1], arrived[1], 1)
 
-    d_value = d_value.reshape(2, tok, kv_half)
+    d_halves = d_value.reshape(2, tok, kv_half)
     part, part_send = [
-        dotted(lax.dynamic_index_in_dim(d_value, which, 0, False), weight_half, ((1,), (1,)))
+        dotted(lax.dynamic_index_in_dim(d_halves, which, 0, False), weight_half, ((1,), (1,))).astype(BF)
         for which in (core, 1 - core)
     ]
-    part_arrived = exchanged(part_send.astype(BF), 1)
-    part, part_arrived = lax.optimization_barrier((part, part_arrived))
-    grad_hidden = (part + part_arrived).astype(BF)
+    part_arrived = exchanged(part_send, 1)
+    grad_hidden = (part.astype(F32) + part_arrived.astype(F32)).astype(BF)
 
     kept, dk, attention, grad_queries, grad_hidden, *terms = lax.optimization_barrier(
         (kept, dk_parts[0], attention, grad_queries, grad_hidden, *terms)

time: 79.8 us -> 90.2 us (1.13)
  the two profiles are of different devices: /device:TPU:6 before, /device:TPU:3 now
where the time goes in v3:
time: 90.2 us; the launch traced here: 89.9 us
  starting transfers between devices  39.7 us (44%)
  waiting for transfers between devices  22.6 us (25%)
  Pallas kernels  15 us (17%)
  local copies, waits for them, and re-layouts  4.88 us (5%)
  other arithmetic  4.52 us (5%)
  matrix products  2.24 us (2%)
  between operations  1.01 us (1%)
    ppermute x19, starting transfers between devices, exchanged(): lax.ppermute(block, 'seq', [(i, i ^ mask) for i in range(lax.axis_size('s...  28.1 us
    ppermute x19, waiting for transfers between devices, exchanged(): lax.ppermute(block, 'seq', [(i, i ^ mask) for i in range(lax.axis_size('s...  22.5 us
    ppermute x8, starting transfers between devices, passed_along(): lax.ppermute(block, 'seq', [(i, (i + distance) % n) for i in range(n)])  11.6 us
    pallas_call x1, Pallas kernels, step(): pl.pallas_call(functools.partial(backward_kernel, tok=tok, reach=reach),...  5.43 us
    pallas_call x1, Pallas kernels, step(): pl.pallas_call(functools.partial(forward_kernel, tok=tok, reach=reach), g...  5.22 us
    unnamed x46, local copies, waits for them, and re-layouts  3.69 us
    pallas_call x1, Pallas kernels, chip_values(): pl.pallas_call(functools.partial(value_kernel, digits=digits, rows=rows),...  2.69 us
    concatenate x4, other arithmetic, in_core_order(): return jnp.concatenate([first, second], axis)  2.33 us
  transfers between devices with their start and end apart: 27, of which 9 were waited for; matrix products, arithmetic and copies ran while one was open for 8% of the time, Pallas kernels for 15%

profile of v3, /device:TPU:3, one launch (start us, length us, event | category | flops | bytes accessed | tf_op | source)
XLA Modules:
  0.0 89.9 jit_solution(7758457209906170257)
XLA Ops:
  0.6 1.7 %first.1 = bf16[192,256]{1,0:T(8,128)(2,1)} custom-call(s32[1]{0:T(128)} %bitcast.place, bf16[128,512]{1,0:T(8,128)(2,1)} %key_ref.1, f32[64,512]{1,0:T(8,128)} %weight_ref.1), custom_call_target="tpu_custom_call" | custom-call | bytes 262144 | tf_op jit(solution)/shard_map/first/pallas_call | solution.py:218
  5.0 3.4 %collective-permute-start.12 = (bf16[1,128,256]{2,1,0:T(8,128)(2,1)S(1)}, bf16[1,128,256]{2,1,0:T(8,128)(2,1)S(1)}, u32[]{:S(2)}, u32[]{:S(2)}) collective-permute-start(bf16[1,128,256]{2,1,0:T(8,128)(2,1)S(1)} %get-tuple-element.69), channel_id=1, source_target_pairs={{0,24},{1,25},{2,26},{3,27},{4,28},{5,29},{6,30},{7,31},{8,16},{9,... | collective-permute-start | bytes 196616 | tf_op jit(solution)/shard_map/ppermute | solution.py:31
  8.8 1.2 %collective-permute-start.1 = (bf16[128,2048]{1,0:T(8,128)(2,1)S(1)}, bf16[128,2048]{1,0:T(8,128)(2,1)S(1)}, u32[]{:S(2)}, u32[]{:S(2)}) collective-permute-start(bf16[128,2048]{1,0:T(8,128)(2,1)S(1)} %pad_maximum_fusion), channel_id=1, source_target_pairs={{0,1},{1,0},{2,3},{3,2},{4,5},{5,4},{6,7},{7,6},{8,9},{9,8},{10,11... | collective-permute-start | bytes 1572872 | tf_op jit(solution)/shard_map/ppermute | solution.py:31
  10.1 3.0 %collective-permute-done.10 = bf16[1,128,256]{2,1,0:T(8,128)(2,1)S(1)} collective-permute-done((bf16[1,128,256]{2,1,0:T(8,128)(2,1)S(1)}, bf16[1,128,256]{2,1,0:T(8,128)(2,1)S(1)}, u32[]{:S(2)}, u32[]{:S(2)}) %collective-permute-start.10) | collective-permute-done | bytes 65568 | tf_op jit(solution)/shard_map/ppermute | solution.py:31
  13.2 1.5 %collective-permute-start.14 = (bf16[4,128,256]{2,1,0:T(8,128)(2,1)S(1)}, bf16[4,128,256]{2,1,0:T(8,128)(2,1)S(1)}, u32[]{:S(2)}, u32[]{:S(2)}) collective-permute-start(bf16[4,128,256]{2,1,0:T(8,128)(2,1)S(1)} %maximum_bitcast_fusion.refs_0_), channel_id=1, source_target_pairs={{0,4},{1,5},{2,6},{3,7},{4,0},{5,1},{6,2},{7,3},{8,12},{9,13},{10,... | collective-permute-start | bytes 786440 | tf_op jit(solution)/shard_map/ppermute | solution.py:31
  14.7 1.2 %collective-permute-start.15 = (bf16[4,128,256]{2,1,0:T(8,128)(2,1)S(1)}, bf16[4,128,256]{2,1,0:T(8,128)(2,1)S(1)}, u32[]{:S(2)}, u32[]{:S(2)}) collective-permute-start(bf16[4,128,256]{2,1,0:T(8,128)(2,1)S(1)} %maximum_bitcast_fusion.refs_0_), channel_id=1, source_target_pairs={{0,6},{1,7},{2,4},{3,5},{4,2},{5,3},{6,0},{7,1},{8,14},{9,15},{10,... | collective-permute-start | bytes 786440 | tf_op jit(solution)/shard_map/ppermute | solution.py:31
  15.9 3.3 %collective-permute-done.13.refs_1_ = bf16[4,128,256]{2,1,0:T(8,128)(2,1)S(1)} collective-permute-done((bf16[4,128,256]{2,1,0:T(8,128)(2,1)S(1)}, bf16[4,128,256]{2,1,0:T(8,128)(2,1)S(1)}, u32[]{:S(2)}, u32[]{:S(2)}) %collective-permute-start.13) | collective-permute-done | bytes 262176 | tf_op jit(solution)/shard_map/ppermute | solution.py:31
  19.2 1.2 %collective-permute-start.3 = (bf16[256,256]{1,0:T(8,128)(2,1)S(1)}, bf16[256,256]{1,0:T(8,128)(2,1)S(1)}, u32[]{:S(2)}, u32[]{:S(2)}) collective-permute-start(bf16[256,256]{1,0:T(8,128)(2,1)S(1)} %pad_maximum_fusion.3.refs_2_), channel_id=1, source_target_pairs={{0,4},{1,5},{2,6},{3,7},{4,8},{5,9},{6,10},{7,11},{8,12},{9,13},{1... | collective-permute-start | bytes 393224 | tf_op jit(solution)/shard_map/ppermute | solution.py:36
  20.4 3.5 %collective-permute-start.4 = (bf16[256,256]{1,0:T(8,128)(2,1)S(1)}, bf16[256,256]{1,0:T(8,128)(2,1)S(1)}, u32[]{:S(2)}, u32[]{:S(2)}) collective-permute-start(bf16[256,256]{1,0:T(8,128)(2,1)S(1)} %pad_maximum_fusion.3.refs_2_), channel_id=1, source_target_pairs={{0,2},{1,3},{2,4},{3,5},{4,6},{5,7},{6,8},{7,9},{8,10},{9,11},{10,... | collective-permute-start | bytes 393224 | tf_op jit(solution)/shard_map/ppermute | solution.py:36
  23.9 2.5 %collective-permute-done.15.refs_3_ = bf16[4,128,256]{2,1,0:T(8,128)(2,1)S(1)} collective-permute-done((bf16[4,128,256]{2,1,0:T(8,128)(2,1)S(1)}, bf16[4,128,256]{2,1,0:T(8,128)(2,1)S(1)}, u32[]{:S(2)}, u32[]{:S(2)}) %collective-permute-start.15) | collective-permute-done | bytes 262176 | tf_op jit(solution)/shard_map/ppermute | solution.py:31
  28.0 2.7 %values.1 = (bf16[256,256]{1,0:T(8,128)(2,1)}, bf16[2048,256]{1,0:T(8,128)(2,1)}) custom-call(s32[1]{0:T(128)} %bitcast.place, bf16[128,2048]{1,0:T(8,128)(2,1)} %h_own.1, bf16[128,2048]{1,0:T(8,128)(2,1)} %copy-done.2, bf16[4,128,256]{2,1,0:T(8,128)(2,1)} %copy-done.5, bf16[4,128,256]{2,1,0:T(8,128)(2,1)} %copy-done.10, bf16[4,128,256]{2,1,0:T(8,128)(2,1)} %copy-done.11, ...), custom_call_target="tpu_custom_call" | custom-call | flops 268435456 | bytes 3145728 | tf_op jit(solution)/shard_map/values/pallas_call | solution.py:165
  30.7 2.8 %collective-permute-start.17 = (bf16[256,256]{1,0:T(8,128)(2,1)}, bf16[256,256]{1,0:T(8,128)(2,1)S(1)}, u32[]{:S(2)}, u32[]{:S(2)}) collective-permute-start(bf16[256,256]{1,0:T(8,128)(2,1)} %get-tuple-element.29.refs_5_), channel_id=1, source_target_pairs={{0,2},{1,3},{2,4},{3,5},{4,6},{5,7},{6,8},{7,9},{8,10},{9,11},{10,... | collective-permute-start | bytes 393224 | tf_op jit(solution)/shard_map/ppermute | solution.py:36
  35.0 5.2 %probs.1 = (bf16[2,2,640,512]{3,2,1,0:T(8,128)(2,1)}, f32[256,256]{1,0:T(8,128)}, bf16[256,256]{1,0:T(8,128)(2,1)}, bf16[256,256]{1,0:T(8,128)(2,1)}) custom-call(s32[1]{0:T(128)} %bitcast.place, bf16[128,2048]{1,0:T(8,128)(2,1)} %q_own.3, bf16[128,2048]{1,0:T(8,128)(2,1)} %copy-done.4, bf16[128,2048]{1,0:T(8,128)(2,1)} %g_own.3, ...), custom_call_target="tpu_custom_call" | custom-call | flops 671088640 | bytes 8388608 | tf_op jit(solution)/shard_map/probs/pallas_call | solution.py:265
  40.2 2.8 %collective-permute-start.6 = (bf16[256,256]{1,0:T(8,128)(2,1)}, bf16[256,256]{1,0:T(8,128)(2,1)S(1)}, u32[]{:S(2)}, u32[]{:S(2)}) collective-permute-start(bf16[256,256]{1,0:T(8,128)(2,1)} %get-tuple-element.28), channel_id=1, source_target_pairs={{0,28},{1,29},{2,30},{3,31},{4,0},{5,1},{6,2},{7,3},{8,4},{9,5},{1... | collective-permute-start | bytes 393224 | tf_op jit(solution)/shard_map/ppermute | solution.py:36
  43.9 5.4 %gradients.1 = (bf16[2,128,1024]{2,1,0:T(8,128)(2,1)}, bf16[2,128,1024]{2,1,0:T(8,128)(2,1)}, f32[256,256]{1,0:T(8,128)}, bf16[256,256]{1,0:T(8,128)(2,1)}, bf16[256,256]{1,0:T(8,128)(2,1)}) custom-call(s32[1]{0:T(128)} %bitcast.place, bf16[128,2048]{1,0:T(8,128)(2,1)} %q_own.3, bf16[128,2048]{1,0:T(8,128)(2,1)} %copy-done.4, bf16[128,2048]{1,0:T(8,128)(2,1)} %g_own.3, ...), custom_call_target="tpu_custom_call" | custom-call | flops 1342177280 | bytes 8388608 | tf_op jit(solution)/shard_map/gradients/pallas_call | solution.py:304
  49.3 7.8 %collective-permute-start.18 = (bf16[2,128,1024]{2,1,0:T(8,128)(2,1)}, bf16[2,128,1024]{2,1,0:T(8,128)(2,1)S(1)}, u32[]{:S(2)}, u32[]{:S(2)}) collective-permute-start(bf16[2,128,1024]{2,1,0:T(8,128)(2,1)} %get-tuple-element.33), channel_id=1, source_target_pairs={{0,1},{1,0},{2,3},{3,2},{4,5},{5,4},{6,7},{7,6},{8,9},{9,8},{10,11... | collective-permute-start | bytes 1572872 | tf_op jit(solution)/shard_map/ppermute | solution.py:31
  57.8 1.2 %collective-permute-start.7 = (bf16[4,128,256]{2,1,0:T(8,128)(2,1)S(1)}, bf16[4,128,256]{2,1,0:T(8,128)(2,1)S(1)}, u32[]{:S(2)}, u32[]{:S(2)}) collective-permute-start(bf16[4,128,256]{2,1,0:T(8,128)(2,1)S(1)} %get-tuple-element.52), channel_id=1, source_target_pairs={{0,2},{1,3},{2,0},{3,1},{4,6},{5,7},{6,4},{7,5},{8,10},{9,11},{10,... | collective-permute-start | bytes 786440 | tf_op jit(solution)/shard_map/ppermute | solution.py:31
  59.0 1.5 %collective-permute-start.9 = (bf16[4,128,256]{2,1,0:T(8,128)(2,1)S(1)}, bf16[4,128,256]{2,1,0:T(8,128)(2,1)S(1)}, u32[]{:S(2)}, u32[]{:S(2)}) collective-permute-start(bf16[4,128,256]{2,1,0:T(8,128)(2,1)S(1)} %get-tuple-element.53), channel_id=1, source_target_pairs={{0,6},{1,7},{2,4},{3,5},{4,2},{5,3},{6,0},{7,1},{8,14},{9,15},{10,... | collective-permute-start | bytes 786440 | tf_op jit(solution)/shard_map/ppermute | solution.py:31
  61.9 3.8 %collective-permute-done.7 = bf16[4,128,256]{2,1,0:T(8,128)(2,1)S(1)} collective-permute-done((bf16[4,128,256]{2,1,0:T(8,128)(2,1)S(1)}, bf16[4,128,256]{2,1,0:T(8,128)(2,1)S(1)}, u32[]{:S(2)}, u32[]{:S(2)}) %collective-permute-start.7) | collective-permute-done | bytes 262176 | tf_op jit(solution)/shard_map/ppermute | solution.py:31
  65.7 1.2 %collective-permute-start.23 = (bf16[256,256]{1,0:T(8,128)(2,1)S(1)}, bf16[256,256]{1,0:T(8,128)(2,1)S(1)}, u32[]{:S(2)}, u32[]{:S(2)}) collective-permute-start(bf16[256,256]{1,0:T(8,128)(2,1)S(1)} %copy-done.22), channel_id=1, source_target_pairs={{0,30},{1,31},{2,0},{3,1},{4,2},{5,3},{6,4},{7,5},{8,6},{9,7},{10,... | collective-permute-start | bytes 393224 | tf_op jit(solution)/shard_map/ppermute | solution.py:36
  66.9 8.1 %collective-permute-done.8 = bf16[4,128,256]{2,1,0:T(8,128)(2,1)S(1)} collective-permute-done((bf16[4,128,256]{2,1,0:T(8,128)(2,1)S(1)}, bf16[4,128,256]{2,1,0:T(8,128)(2,1)S(1)}, u32[]{:S(2)}, u32[]{:S(2)}) %collective-permute-start.8) | collective-permute-done | bytes 262176 | tf_op jit(solution)/shard_map/ppermute | solution.py:31
  77.2 2.6 %collective-permute-start.22 = (bf16[1,128,256]{2,1,0:T(8,128)(2,1)S(1)}, bf16[1,128,256]{2,1,0:T(8,128)(2,1)S(1)}, u32[]{:S(2)}, u32[]{:S(2)}) collective-permute-start(bf16[1,128,256]{2,1,0:T(8,128)(2,1)S(1)} %get-tuple-element.57), channel_id=1, source_target_pairs={{0,24},{1,25},{2,26},{3,27},{4,28},{5,29},{6,30},{7,31},{8,16},{9,... | collective-permute-start | bytes 196616 | tf_op jit(solution)/shard_map/ppermute | solution.py:31
  79.8 1.3 %fusion.2 = bf16[128,2048]{1,0:T(8,128)(2,1)} fusion(bf16[2048,256]{1,0:T(8,128)(2,1)S(1)} %copy-done, bf16[128,2048]{1,0:T(8,128)(2,1)S(1)} %collective-permute-done.19, bf16[2,128,256]{2,1,0:T(8,128)(2,1)S(1)} %bitcast.53, s32[]{:T(128)S(6)} %select_n.157), kind=kOutput, calls=%fused_computation.5 | convolution fusion | flops 135528448 | bytes 2162692 | tf_op jit(solution)/shard_map/dot_general | solution.py:55
  82.9 4.5 %collective-permute-start.25 = (bf16[128,256]{1,0:T(8,128)(2,1)S(1)}, bf16[128,256]{1,0:T(8,128)(2,1)S(1)}, u32[]{:S(2)}, u32[]{:S(2)}) collective-permute-start(bf16[128,256]{1,0:T(8,128)(2,1)S(1)} %dynamic-slice_bitcast_fusion.4), channel_id=1, source_target_pairs={{0,1},{1,0},{2,3},{3,2},{4,5},{5,4},{6,7},{7,6},{8,9},{9,8},{10,11... | collective-permute-start | bytes 196616 | tf_op jit(solution)/shard_map/ppermute | solution.py:31
  (107 shorter events, 15.6 us)
Async XLA Ops:
  3.0 23.5 %collective-permute-start = (bf16[128,2048]{1,0:T(8,128)(2,1)}, bf16[128,2048]{1,0:T(8,128)(2,1)S(1)}, u32[]{:S(2)}, u32[]{:S(2)}) collective-permute-start(bf16[128,2048]{1,0:T(8,128)(2,1)} %h_own.1), channel_id=1, source_target_pairs={{0,1},{1,0},{2,3},{3,2},{4,5},{5,4},{6,7},{7,6},{8,9},{9,8},{10,11... | collective-permute-start | bytes 1572872 | tf_op jit(solution)/shard_map/ppermute | solution.py:31
  5.0 5.1 %collective-permute-start.12 = (bf16[1,128,256]{2,1,0:T(8,128)(2,1)S(1)}, bf16[1,128,256]{2,1,0:T(8,128)(2,1)S(1)}, u32[]{:S(2)}, u32[]{:S(2)}) collective-permute-start(bf16[1,128,256]{2,1,0:T(8,128)(2,1)S(1)} %get-tuple-element.69), channel_id=1, source_target_pairs={{0,24},{1,25},{2,26},{3,27},{4,28},{5,29},{6,30},{7,31},{8,16},{9,... | collective-permute-start | bytes 196616 | tf_op jit(solution)/shard_map/ppermute | solution.py:31
  8.4 4.7 %collective-permute-start.11 = (bf16[1,128,256]{2,1,0:T(8,128)(2,1)S(1)}, bf16[1,128,256]{2,1,0:T(8,128)(2,1)S(1)}, u32[]{:S(2)}, u32[]{:S(2)}) collective-permute-start(bf16[1,128,256]{2,1,0:T(8,128)(2,1)S(1)} %get-tuple-element.69), channel_id=1, source_target_pairs={{0,16},{1,17},{2,18},{3,19},{4,20},{5,21},{6,22},{7,23},{8,24},{9,... | collective-permute-start | bytes 196616 | tf_op jit(solution)/shard_map/ppermute | solution.py:31
  8.8 24.7 %collective-permute-start.1 = (bf16[128,2048]{1,0:T(8,128)(2,1)S(1)}, bf16[128,2048]{1,0:T(8,128)(2,1)S(1)}, u32[]{:S(2)}, u32[]{:S(2)}) collective-permute-start(bf16[128,2048]{1,0:T(8,128)(2,1)S(1)} %pad_maximum_fusion), channel_id=1, source_target_pairs={{0,1},{1,0},{2,3},{3,2},{4,5},{5,4},{6,7},{7,6},{8,9},{9,8},{10,11... | collective-permute-start | bytes 1572872 | tf_op jit(solution)/shard_map/ppermute | solution.py:31
  13.1 6.0 %collective-permute-start.13 = (bf16[4,128,256]{2,1,0:T(8,128)(2,1)S(1)}, bf16[4,128,256]{2,1,0:T(8,128)(2,1)S(1)}, u32[]{:S(2)}, u32[]{:S(2)}) collective-permute-start(bf16[4,128,256]{2,1,0:T(8,128)(2,1)S(1)} %maximum_bitcast_fusion.refs_0_), channel_id=1, source_target_pairs={{0,2},{1,3},{2,0},{3,1},{4,6},{5,7},{6,4},{7,5},{8,10},{9,11},{10,... | collective-permute-start | bytes 786440 | tf_op jit(solution)/shard_map/ppermute | solution.py:31
  13.2 7.2 %collective-permute-start.14 = (bf16[4,128,256]{2,1,0:T(8,128)(2,1)S(1)}, bf16[4,128,256]{2,1,0:T(8,128)(2,1)S(1)}, u32[]{:S(2)}, u32[]{:S(2)}) collective-permute-start(bf16[4,128,256]{2,1,0:T(8,128)(2,1)S(1)} %maximum_bitcast_fusion.refs_0_), channel_id=1, source_target_pairs={{0,4},{1,5},{2,6},{3,7},{4,0},{5,1},{6,2},{7,3},{8,12},{9,13},{10,... | collective-permute-start | bytes 786440 | tf_op jit(solution)/shard_map/ppermute | solution.py:31
  14.7 11.7 %collective-permute-start.15 = (bf16[4,128,256]{2,1,0:T(8,128)(2,1)S(1)}, bf16[4,128,256]{2,1,0:T(8,128)(2,1)S(1)}, u32[]{:S(2)}, u32[]{:S(2)}) collective-permute-start(bf16[4,128,256]{2,1,0:T(8,128)(2,1)S(1)} %maximum_bitcast_fusion.refs_0_), channel_id=1, source_target_pairs={{0,6},{1,7},{2,4},{3,5},{4,2},{5,3},{6,0},{7,1},{8,14},{9,15},{10,... | collective-permute-start | bytes 786440 | tf_op jit(solution)/shard_map/ppermute | solution.py:31
  19.2 14.3 %collective-permute-start.3 = (bf16[256,256]{1,0:T(8,128)(2,1)S(1)}, bf16[256,256]{1,0:T(8,128)(2,1)S(1)}, u32[]{:S(2)}, u32[]{:S(2)}) collective-permute-start(bf16[256,256]{1,0:T(8,128)(2,1)S(1)} %pad_maximum_fusion.3.refs_2_), channel_id=1, source_target_pairs={{0,4},{1,5},{2,6},{3,7},{4,8},{5,9},{6,10},{7,11},{8,12},{9,13},{1... | collective-permute-start | bytes 393224 | tf_op jit(solution)/shard_map/ppermute | solution.py:36
  20.4 13.1 %collective-permute-start.4 = (bf16[256,256]{1,0:T(8,128)(2,1)S(1)}, bf16[256,256]{1,0:T(8,128)(2,1)S(1)}, u32[]{:S(2)}, u32[]{:S(2)}) collective-permute-start(bf16[256,256]{1,0:T(8,128)(2,1)S(1)} %pad_maximum_fusion.3.refs_2_), channel_id=1, source_target_pairs={{0,2},{1,3},{2,4},{3,5},{4,6},{5,7},{6,8},{7,9},{8,10},{9,11},{10,... | collective-permute-start | bytes 393224 | tf_op jit(solution)/shard_map/ppermute | solution.py:36
  30.6 12.5 %collective-permute-start.16 = (bf16[256,256]{1,0:T(8,128)(2,1)}, bf16[256,256]{1,0:T(8,128)(2,1)S(1)}, u32[]{:S(2)}, u32[]{:S(2)}) collective-permute-start(bf16[256,256]{1,0:T(8,128)(2,1)} %get-tuple-element.29.refs_5_), channel_id=1, source_target_pairs={{0,4},{1,5},{2,6},{3,7},{4,8},{5,9},{6,10},{7,11},{8,12},{9,13},{1... | collective-permute-start | bytes 393224 | tf_op jit(solution)/shard_map/ppermute | solution.py:36
  30.7 12.5 %collective-permute-start.17 = (bf16[256,256]{1,0:T(8,128)(2,1)}, bf16[256,256]{1,0:T(8,128)(2,1)S(1)}, u32[]{:S(2)}, u32[]{:S(2)}) collective-permute-start(bf16[256,256]{1,0:T(8,128)(2,1)} %get-tuple-element.29.refs_5_), channel_id=1, source_target_pairs={{0,2},{1,3},{2,4},{3,5},{4,6},{5,7},{6,8},{7,9},{8,10},{9,11},{10,... | collective-permute-start | bytes 393224 | tf_op jit(solution)/shard_map/ppermute | solution.py:36
  40.2 16.9 %collective-permute-start.5 = (bf16[256,256]{1,0:T(8,128)(2,1)}, bf16[256,256]{1,0:T(8,128)(2,1)S(1)}, u32[]{:S(2)}, u32[]{:S(2)}) collective-permute-start(bf16[256,256]{1,0:T(8,128)(2,1)} %get-tuple-element.27), channel_id=1, source_target_pairs={{0,30},{1,31},{2,0},{3,1},{4,2},{5,3},{6,4},{7,5},{8,6},{9,7},{10,... | collective-permute-start | bytes 393224 | tf_op jit(solution)/shard_map/ppermute | solution.py:36
  40.2 16.9 %collective-permute-start.6 = (bf16[256,256]{1,0:T(8,128)(2,1)}, bf16[256,256]{1,0:T(8,128)(2,1)S(1)}, u32[]{:S(2)}, u32[]{:S(2)}) collective-permute-start(bf16[256,256]{1,0:T(8,128)(2,1)} %get-tuple-element.28), channel_id=1, source_target_pairs={{0,28},{1,29},{2,30},{3,31},{4,0},{5,1},{6,2},{7,3},{8,4},{9,5},{1... | collective-permute-start | bytes 393224 | tf_op jit(solution)/shard_map/ppermute | solution.py:36
  49.3 26.2 %collective-permute-start.18 = (bf16[2,128,1024]{2,1,0:T(8,128)(2,1)}, bf16[2,128,1024]{2,1,0:T(8,128)(2,1)S(1)}, u32[]{:S(2)}, u32[]{:S(2)}) collective-permute-start(bf16[2,128,1024]{2,1,0:T(8,128)(2,1)} %get-tuple-element.33), channel_id=1, source_target_pairs={{0,1},{1,0},{2,3},{3,2},{4,5},{5,4},{6,7},{7,6},{8,9},{9,8},{10,11... | collective-permute-start | bytes 1572872 | tf_op jit(solution)/shard_map/ppermute | solution.py:31
  57.8 7.9 %collective-permute-start.7 = (bf16[4,128,256]{2,1,0:T(8,128)(2,1)S(1)}, bf16[4,128,256]{2,1,0:T(8,128)(2,1)S(1)}, u32[]{:S(2)}, u32[]{:S(2)}) collective-permute-start(bf16[4,128,256]{2,1,0:T(8,128)(2,1)S(1)} %get-tuple-element.52), channel_id=1, source_target_pairs={{0,2},{1,3},{2,0},{3,1},{4,6},{5,7},{6,4},{7,5},{8,10},{9,11},{10,... | collective-permute-start | bytes 786440 | tf_op jit(solution)/shard_map/ppermute | solution.py:31
  59.0 16.0 %collective-permute-start.8 = (bf16[4,128,256]{2,1,0:T(8,128)(2,1)S(1)}, bf16[4,128,256]{2,1,0:T(8,128)(2,1)S(1)}, u32[]{:S(2)}, u32[]{:S(2)}) collective-permute-start(bf16[4,128,256]{2,1,0:T(8,128)(2,1)S(1)} %get-tuple-element.54), channel_id=1, source_target_pairs={{0,4},{1,5},{2,6},{3,7},{4,0},{5,1},{6,2},{7,3},{8,12},{9,13},{10,... | collective-permute-start | bytes 786440 | tf_op jit(solution)/shard_map/ppermute | solution.py:31
  59.0 16.0 %collective-permute-start.9 = (bf16[4,128,256]{2,1,0:T(8,128)(2,1)S(1)}, bf16[4,128,256]{2,1,0:T(8,128)(2,1)S(1)}, u32[]{:S(2)}, u32[]{:S(2)}) collective-permute-start(bf16[4,128,256]{2,1,0:T(8,128)(2,1)S(1)} %get-tuple-element.53), channel_id=1, source_target_pairs={{0,6},{1,7},{2,4},{3,5},{4,2},{5,3},{6,0},{7,1},{8,14},{9,15},{10,... | collective-permute-start | bytes 786440 | tf_op jit(solution)/shard_map/ppermute | solution.py:31
  61.0 16.2 %collective-permute-start.19 = (bf16[128,2048]{1,0:T(8,128)(2,1)S(1)}, bf16[128,2048]{1,0:T(8,128)(2,1)S(1)}, u32[]{:S(2)}, u32[]{:S(2)}) collective-permute-start(bf16[128,2048]{1,0:T(8,128)(2,1)S(1)} %convolution_convert_fusion.1), channel_id=1, source_target_pairs={{0,1},{1,0},{2,3},{3,2},{4,5},{5,4},{6,7},{7,6},{8,9},{9,8},{10,11... | collective-permute-start | bytes 1572872 | tf_op jit(solution)/shard_map/ppermute | solution.py:31
  65.7 17.2 %collective-permute-start.23 = (bf16[256,256]{1,0:T(8,128)(2,1)S(1)}, bf16[256,256]{1,0:T(8,128)(2,1)S(1)}, u32[]{:S(2)}, u32[]{:S(2)}) collective-permute-start(bf16[256,256]{1,0:T(8,128)(2,1)S(1)} %copy-done.22), channel_id=1, source_target_pairs={{0,30},{1,31},{2,0},{3,1},{4,2},{5,3},{6,4},{7,5},{8,6},{9,7},{10,... | collective-permute-start | bytes 393224 | tf_op jit(solution)/shard_map/ppermute | solution.py:36
  75.0 7.9 %collective-permute-start.24 = (bf16[256,256]{1,0:T(8,128)(2,1)S(1)}, bf16[256,256]{1,0:T(8,128)(2,1)S(1)}, u32[]{:S(2)}, u32[]{:S(2)}) collective-permute-start(bf16[256,256]{1,0:T(8,128)(2,1)S(1)} %copy-done.21), channel_id=1, source_target_pairs={{0,28},{1,29},{2,30},{3,31},{4,0},{5,1},{6,2},{7,3},{8,4},{9,5},{1... | collective-permute-start | bytes 393224 | tf_op jit(solution)/shard_map/ppermute | solution.py:36
  75.2 6.7 %collective-permute-start.20 = (bf16[1,128,256]{2,1,0:T(8,128)(2,1)S(1)}, bf16[1,128,256]{2,1,0:T(8,128)(2,1)S(1)}, u32[]{:S(2)}, u32[]{:S(2)}) collective-permute-start(bf16[1,128,256]{2,1,0:T(8,128)(2,1)S(1)} %get-tuple-element.59), channel_id=1, source_target_pairs={{0,8},{1,9},{2,10},{3,11},{4,12},{5,13},{6,14},{7,15},{8,0},{9,1},... | collective-permute-start | bytes 196616 | tf_op jit(solution)/shard_map/ppermute | solution.py:31
  75.6 6.4 %collective-permute-start.21 = (bf16[1,128,256]{2,1,0:T(8,128)(2,1)S(1)}, bf16[1,128,256]{2,1,0:T(8,128)(2,1)S(1)}, u32[]{:S(2)}, u32[]{:S(2)}) collective-permute-start(bf16[1,128,256]{2,1,0:T(8,128)(2,1)S(1)} %get-tuple-element.58), channel_id=1, source_target_pairs={{0,16},{1,17},{2,18},{3,19},{4,20},{5,21},{6,22},{7,23},{8,24},{9,... | collective-permute-start | bytes 196616 | tf_op jit(solution)/shard_map/ppermute | solution.py:31
  77.2 5.6 %collective-permute-start.22 = (bf16[1,128,256]{2,1,0:T(8,128)(2,1)S(1)}, bf16[1,128,256]{2,1,0:T(8,128)(2,1)S(1)}, u32[]{:S(2)}, u32[]{:S(2)}) collective-permute-start(bf16[1,128,256]{2,1,0:T(8,128)(2,1)S(1)} %get-tuple-element.57), channel_id=1, source_target_pairs={{0,24},{1,25},{2,26},{3,27},{4,28},{5,29},{6,30},{7,31},{8,16},{9,... | collective-permute-start | bytes 196616 | tf_op jit(solution)/shard_map/ppermute | solution.py:31
  82.9 5.4 %collective-permute-start.25 = (bf16[128,256]{1,0:T(8,128)(2,1)S(1)}, bf16[128,256]{1,0:T(8,128)(2,1)S(1)}, u32[]{:S(2)}, u32[]{:S(2)}) collective-permute-start(bf16[128,256]{1,0:T(8,128)(2,1)S(1)} %dynamic-slice_bitcast_fusion.4), channel_id=1, source_target_pairs={{0,1},{1,0},{2,3},{3,2},{4,5},{5,4},{6,7},{7,6},{8,9},{9,8},{10,11... | collective-permute-start | bytes 196616 | tf_op jit(solution)/shard_map/ppermute | solution.py:31
  (26 other events, 188.3 us)
